TPU v7x, 128 devices: a whole 4x4x4 slice. The times are simulated.
128 devices in a mesh: seq: 64 (over x_lo, z, y, core), ch: 2 (over x_hi).
Axes of the slice: x: 4 (x_hi: 2, x_lo: 2; x = x_hi * 2 + x_lo), y: 4, z: 4, core: 2. Of those that a mesh axis runs over, the one named last changes fastest.
Arguments:
- inputs: bfloat16 [4, 16384, 1536], P(None, 'seq', 'ch'), may hold values from -6 to 6
- kernels: float32 [3, 3, 1536], P(None, None, 'ch'), may hold values from -3.5 to 3.5
- mixers: bfloat16 [3, 1536, 1536], P(None, None, 'ch'), may hold values from -0.15625 to 0.15625
- cotangent: bfloat16 [4, 16384, 1536], P(None, 'seq', 'ch'), may hold values from -6 to 6
Outputs:
- outputs: bfloat16 [4, 16384, 1536], P(None, 'seq', 'ch')
- input_grad: bfloat16 [4, 16384, 1536], P(None, 'seq', 'ch')
- mixer_grads: float32 [3, 1536, 1536], P(None, 'seq', 'ch')
All inputs are finite; a program needn't handle non-finite values.
Results may differ from a plain program's by a relative error of at most 0.0075.
Values may be sent and summed in bfloat16 or wider, within the bound.
A program may use at most 128 MiB of HBM per device.

v0:
```python
import math

import jax
import jax.numpy as jnp
from jax import lax
from jax.sharding import PartitionSpec as P

dilations = (2, 4, 8)


def padded_2(block, sides, width):
    for axis, dim in sides:
        count = lax.axis_size(axis)
        forward = [(i, i + 1) for i in range(count - 1)]
        backward = [(target, source) for source, target in forward]
        low = lax.ppermute(
            lax.slice_in_dim(block, block.shape[dim] - width, None, axis=dim), axis, forward
        )
        high = lax.ppermute(lax.slice_in_dim(block, 0, width, axis=dim), axis, backward)
        block = jnp.concatenate([low, block, high], axis=dim)
    return block


def gelu_exact(value):
    return 0.5 * value * (1.0 + jax.scipy.special.erf(value * 0.7071067811865476))


def gelu_slope(value):
    return (
        0.5 * (1.0 + jax.scipy.special.erf(value * 0.7071067811865476))
        + value * jnp.exp(-0.5 * value * value) * 0.3989422804014327
    )


def convolve(padded, kernel, width):
    length = padded.shape[1] - 2 * width
    wide = padded.astype(jnp.float32)
    return (
        kernel[0] * wide[:, 0:length]
        + kernel[1] * wide[:, width : width + length]
        + kernel[2] * wide[:, 2 * width : 2 * width + length]
    )


def mixing(center, act, mixer):
    seqs, length, chans = act.shape
    gathered = lax.all_gather(act.reshape(seqs * length, chans), "ch", axis=1, tiled=True)
    mixed = jnp.dot(gathered, mixer, preferred_element_type=jnp.float32)
    result = (center.astype(jnp.float32) + mixed.reshape(seqs, length, chans)).astype(jnp.bfloat16)
    return (gathered, result)


def on_device(inputs, kernels, mixers, cotangent):
    seqs, bins, chans = inputs.shape
    devices_seq = lax.axis_size("seq")
    saved = []
    current = inputs
    for block, width in enumerate(dilations):
        padded = padded_2(current, (("seq", 1),), width)
        pre = convolve(padded, kernels[block], width)
        act = gelu_exact(pre).astype(jnp.bfloat16)
        gathered, current = mixing(current, act, mixers[block])
        saved.append((pre, gathered))
    scale = 1.0 / math.sqrt(seqs * bins * devices_seq)
    grad_list = [None, None, None]
    upper = cotangent
    for block in (2, 1, 0):
        width = dilations[block]
        kernel = kernels[block]
        pre, gathered = saved[block]
        flat = upper.reshape(seqs * bins, chans)
        term = jnp.einsum("rj,cj->rc", flat, mixers[block], preferred_element_type=jnp.float32)
        back = lax.psum_scatter(term, "ch", scatter_dimension=1, tiled=True)
        slope = (back.reshape(seqs, bins, chans) * gelu_slope(pre)).astype(jnp.bfloat16)
        local_grad = (
            jnp.einsum("rc,rj->cj", gathered, flat, preferred_element_type=jnp.float32) * scale
        )
        grad_list[block] = local_grad
        padded = padded_2(slope, (("seq", 1),), width).astype(jnp.float32)
        lower = (
            upper.astype(jnp.float32)
            + kernel[0] * padded[:, 2 * width : 2 * width + bins]
            + kernel[1] * padded[:, width : width + bins]
            + kernel[2] * padded[:, 0:bins]
        )
        upper = lower.astype(jnp.bfloat16)
    mixer_grads = lax.psum_scatter(jnp.stack(grad_list), "seq", scatter_dimension=1, tiled=True)
    return (current, upper, mixer_grads)


def solution(mesh):
    placed = (P(None, "seq", "ch"), P(None, None, "ch"), P(None, None, "ch"), P(None, "seq", "ch"))
    return jax.shard_map(
        on_device,
        mesh=mesh,
        in_specs=placed,
        out_specs=(P(None, "seq", "ch"), P(None, "seq", "ch"), P(None, "seq", "ch")),
        check_vma=False,
    )
```

profile of v0, /device:TPU:1, one launch (start us, length us, event | category | flops | bytes accessed | tf_op | source)
XLA Modules:
  0.0 778.0 jit_solution(2955091546215567638)
XLA Ops:
  8.1 3.3 collective-permute-start.1
  11.4 3.2 collective-permute-start
  20.4 55.7 %all-gather.4.cloned.1.call-done = bf16[1024,1536]{1,0:T(8,128)(2,1)} async-done(((bf16[1024,768]{1,0:T(8,128)(2,1)}), bf16[1024,1536]{1,0:T(8,128)(2,1)}) %all-gather.4.cloned.1.call-update) | async-done | bytes 3145744 | tf_op jit(solution)/shard_map/all_gather | solution.py:47
  76.1 5.2 add_convert_fusion.2
  91.2 6.2 fusion.38
  97.5 46.8 %all-gather.6.cloned.1.call-done = bf16[1024,1536]{1,0:T(8,128)(2,1)} async-done(((bf16[1024,768]{1,0:T(8,128)(2,1)}), bf16[1024,1536]{1,0:T(8,128)(2,1)}) %all-gather.6.cloned.1.call-update) | async-done | bytes 3145744 | tf_op jit(solution)/shard_map/all_gather | solution.py:47
  144.3 5.2 add_convert_fusion.1
  152.1 3.0 collective-permute-start.4
  156.6 70.7 %reduce-scatter.5.cloned.1.call-done = f32[1024,768]{1,0:T(8,128)} async-done(((f32[1024,1536]{1,0:T(8,128)}), f32[1024,768]{1,0:T(8,128)}) %reduce-scatter.5.cloned.1.call-update) | async-done | bytes 3145744 | tf_op jit(solution)/shard_map/reduce_scatter | solution.py:73
  227.3 4.5 fusion.5
  241.1 6.2 fusion.42
  247.4 3.2 multiply_convert_fusion
  250.8 82.3 %reduce-scatter.7.cloned.1.call-done = f32[1024,768]{1,0:T(8,128)} async-done(((f32[1024,1536]{1,0:T(8,128)}), f32[1024,768]{1,0:T(8,128)}) %reduce-scatter.7.cloned.1.call-update) | async-done | bytes 3145744 | tf_op jit(solution)/shard_map/reduce_scatter | solution.py:73
  338.6 3.0 collective-permute-start.8
  343.9 7.1 fusion.46
  351.1 6.7 multiply_bitcast_fusion.1
  357.8 25.9 %all-gather.8.cloned.1.call-done = bf16[1024,1536]{1,0:T(8,128)(2,1)} async-done(((bf16[1024,768]{1,0:T(8,128)(2,1)}), bf16[1024,1536]{1,0:T(8,128)(2,1)}) %all-gather.8.cloned.1.call-update) | async-done | bytes 3145744 | tf_op jit(solution)/shard_map/all_gather | solution.py:47
  383.6 7.4 multiply_bitcast_fusion
  391.0 4.3 multiply_bitcast_fusion.2
  395.3 11.1 %pad_maximum_fusion = f32[3,1536,768]{2,1,0:T(8,128)} fusion(f32[1,1536,768]{2,1,0:T(8,128)} %multiply_bitcast_fusion, f32[1,1536,768]{2,1,0:T(8,128)} %multiply_bitcast_fusion.1, f32[1,1536,768]{2,1,0:T(8,128)} %multiply_bitcast_fusion.2), kind=kLoop, calls=%fused_computation | loop fusion | flops 7077888 | bytes 28311552 | tf_op jit(solution)/shard_map/stack | solution.py:87
  406.5 59.9 %reduce-scatter.9.cloned.1.call-done = f32[1024,768]{1,0:T(8,128)} async-done(((f32[1024,1536]{1,0:T(8,128)}), f32[1024,768]{1,0:T(8,128)}) %reduce-scatter.9.cloned.1.call-update) | async-done | bytes 3145744 | tf_op jit(solution)/shard_map/reduce_scatter | solution.py:73
  472.0 3.2 collective-permute-start.10
  475.2 5.3 add_convert_fusion
  484.3 286.8 %reduce-scatter.11.cloned.1.call-done = f32[3,24,768]{2,1,0:T(8,128)} async-done(((f32[3,1536,768]{2,1,0:T(8,128)}), f32[3,24,768]{2,1,0:T(8,128)}) %reduce-scatter.11.cloned.1.call-update) | async-done | bytes 221200 | tf_op jit(solution)/shard_map/reduce_scatter | solution.py:87
  (79 shorter events, 47.1 us)
Async XLA Ops:
  7.2 68.9 %all-gather.4.cloned.1.call-start = ((), (), s32[]{:S(2)}) async-start(), calls=%async_computation.4 | async-start | bytes 4718592 | tf_op jit(solution)/shard_map/all_gather | solution.py:47
  8.1 7.5 collective-permute-start.1
  11.4 4.2 collective-permute-start
  17.3 58.8 %copy-start.8 = (bf16[4,256,768]{2,1,0:T(8,128)(2,1)S(1)}, bf16[4,256,768]{2,1,0:T(8,128)(2,1)}, u32[]{:S(2)}) copy-start(bf16[4,256,768]{2,1,0:T(8,128)(2,1)} %param.4) | copy-start | bytes 4718596
  20.3 124.0 %all-gather.6.cloned.1.call-start = ((), (), s32[]{:S(2)}) async-start(), calls=%async_computation.5 | async-start | bytes 4718592 | tf_op jit(solution)/shard_map/all_gather | solution.py:47
  81.4 5.6 collective-permute-start.3
  83.9 3.9 collective-permute-start.2
  91.2 136.1 %reduce-scatter.5.cloned.1.call-start = ((), (), s32[]{:S(2)}) async-start(), calls=%async_computation.7 | async-start | bytes 9437184 | tf_op jit(solution)/shard_map/reduce_scatter | solution.py:73
  97.4 235.7 %reduce-scatter.7.cloned.1.call-start = ((), (), s32[]{:S(2)}) async-start(), calls=%async_computation.8 | async-start | bytes 9437184 | tf_op jit(solution)/shard_map/reduce_scatter | solution.py:73
  149.5 5.6 collective-permute-start.5
  152.1 4.2 collective-permute-start.4
  231.8 5.7 collective-permute-start.7
  234.5 4.2 collective-permute-start.6
  247.3 136.3 %all-gather.8.cloned.1.call-start = ((), (), s32[]{:S(2)}) async-start(), calls=%async_computation.6 | async-start | bytes 4718592 | tf_op jit(solution)/shard_map/all_gather | solution.py:47
  247.3 85.8 %copy-start.1 = (f32[4,256,768]{2,1,0:T(8,128)S(1)}, f32[4,256,768]{2,1,0:T(8,128)}, u32[]{:S(2)}) copy-start(f32[4,256,768]{2,1,0:T(8,128)} %get-tuple-element.15) | copy-start | bytes 9437188
  250.6 215.9 %reduce-scatter.9.cloned.1.call-start = ((), (), s32[]{:S(2)}) async-start(), calls=%async_computation.9 | async-start | bytes 9437184 | tf_op jit(solution)/shard_map/reduce_scatter | solution.py:73
  335.9 5.7 collective-permute-start.9
  338.6 4.0 collective-permute-start.8
  343.9 47.1 %copy-start.4 = (bf16[4,256,768]{2,1,0:T(8,128)(2,1)}, bf16[4,256,768]{2,1,0:T(8,128)(2,1)S(1)}, u32[]{:S(2)}) copy-start(bf16[4,256,768]{2,1,0:T(8,128)(2,1)S(1)} %fusion.23) | copy-start | bytes 4718596
  351.0 420.1 %reduce-scatter.11.cloned.1.call-start = ((), (), s32[]{:S(2)}) async-start(), calls=%async_computation.10 | async-start | bytes 14376960 | tf_op jit(solution)/shard_map/reduce_scatter | solution.py:87
  406.5 60.0 %copy-start = (f32[4,256,768]{2,1,0:T(8,128)S(1)}, f32[4,256,768]{2,1,0:T(8,128)}, u32[]{:S(2)}) copy-start(f32[4,256,768]{2,1,0:T(8,128)} %get-tuple-element.17) | copy-start | bytes 9437188
  466.5 8.8 %copy-start.12 = (bf16[1024,1536]{1,0:T(8,128)(2,1)S(1)}, bf16[1024,1536]{1,0:T(8,128)(2,1)}, u32[]{:S(2)}) copy-start(bf16[1024,1536]{1,0:T(8,128)(2,1)} %all-gather.8.cloned.1.call-done) | copy-start | bytes 9437188
  469.4 11.2 %collective-permute-start.11 = (bf16[4,2,768]{2,1,0:T(2,128)(2,1)S(1)}, bf16[4,2,768]{2,1,0:T(2,128)(2,1)S(1)}, u32[]{:S(2)}, u32[]{:S(2)}) collective-permute-start(bf16[4,2,768]{2,1,0:T(2,128)(2,1)S(1)} %get-tuple-element.19), channel_id=1, source_target_pairs={{2,0},{4,2},{6,4},{8,6},{10,8},{12,10},{14,12},{16,14},{18,16},{20... | collective-permute-start | bytes 36872 | tf_op jit(solution)/shard_map/ppermute | solution.py:19
  472.0 8.6 %collective-permute-start.10 = (bf16[4,2,768]{2,1,0:T(2,128)(2,1)S(1)}, bf16[4,2,768]{2,1,0:T(2,128)(2,1)S(1)}, u32[]{:S(2)}, u32[]{:S(2)}) collective-permute-start(bf16[4,2,768]{2,1,0:T(2,128)(2,1)S(1)} %get-tuple-element.18), channel_id=1, source_target_pairs={{0,2},{2,4},{4,6},{6,8},{8,10},{10,12},{12,14},{14,16},{16,18},{18... | collective-permute-start | bytes 36872 | tf_op jit(solution)/shard_map/ppermute | solution.py:16
  (8 other events, 42.8 us)
Sparse Core Ops, SparseCore 0:
  20.4 55.6 all-gather.3
  91.3 52.9 all-gather.5
  146.7 80.5 reduce-scatter.4
  247.4 85.6 reduce-scatter.6
  335.2 48.3 all-gather.7
  385.9 80.5 reduce-scatter.8
  469.6 301.5 reduce-scatter.10
where the time goes:
time: 784 us; the launch traced here: 778 us
  waiting for transfers between devices  632 us (81%)
  matrix products  53.6 us (7%)
  other arithmetic  37.8 us (5%)
  starting transfers between devices  35.4 us (5%)
  between operations  14.5 us (2%)
    reduce_scatter x1, waiting for transfers between devices, on_device(): lax.psum_scatter(jnp.stack(grad_list), 'seq', scatter_dimension=1, tiled=...  287 us
    reduce_scatter x3, waiting for transfers between devices, on_device(): back = lax.psum_scatter(term, 'ch', scatter_dimension=1, tiled=True)  213 us
    all_gather x3, waiting for transfers between devices, mixing(): lax.all_gather(act.reshape(seqs * length, chans), 'ch', axis=1, tiled=True)  128 us
    dot_general x3, matrix products, on_device(): jnp.einsum('rj,cj->rc', flat, mixers[block], preferred_element_type=jnp.f...  19.5 us
    ppermute x6, starting transfers between devices, padded_2(): lax.ppermute(lax.slice_in_dim(block, block.shape[dim] - width, None, axis...  18.5 us
    dot_general x3, matrix products, on_device(): jnp.einsum('rc,rj->cj', gathered, flat, preferred_element_type=jnp.float32)  18.4 us
    ppermute x6, starting transfers between devices, padded_2(): lax.ppermute(lax.slice_in_dim(block, 0, width, axis=dim), axis, backward)  16.5 us
    dot_general x3, matrix products, mixing(): mixed = jnp.dot(gathered, mixer, preferred_element_type=jnp.float32)  15.8 us
  transfers between devices with their start and end apart: 19, of which 11 were waited for; matrix products, arithmetic and copies ran while one was open for 9% of the time, Pallas kernels for 0%

commit v1 on v0

v1 whole, which is shorter than its diff:
```python
import jax
import jax.numpy as jnp
from jax import lax
from jax.experimental import pallas as pl
from jax.experimental.pallas import tpu as pltpu
from jax.sharding import PartitionSpec as P

dilations = (2, 4, 8)
MESH = pl.DeviceIdType.MESH
ANY = pl.BlockSpec(memory_space=pl.ANY)
bf16, f32 = jnp.bfloat16, jnp.float32
XH, EH = 32, 16
BINS, HALF, FULL = 256, 768, 1536


def place():
    s = lax.axis_index("seq")
    h = lax.axis_index("ch")
    core = lax.rem(s, 2)
    y = lax.rem(s // 2, 4)
    z = lax.rem(s // 8, 4)
    return s, h, s // 32, z, y, core


def other(s):
    return lax.rem(s + 32, 64)


def line(core, low, a, b):
    z = a + core * (b - a)
    y = b + core * (a - b)
    return low * 32 + z * 8 + y * 2 + core


def remote(src, dst, send, recv, to):
    return pltpu.make_async_remote_copy(
        src_ref=src, dst_ref=dst, send_sem=send, recv_sem=recv, device_id=to, device_id_type=MESH
    )


def in_kernel(x_ref, e_ref, m_ref, k_ref, xo, eo, mo, ko, xs, xr, ms, mr, ls):
    s, h, low, z, y, core = place()
    g = other(s)
    cols = pl.ds(pl.multiple_of(h * HALF, HALF), HALF)
    opp = pl.ds(pl.multiple_of((1 - h) * HALF, HALF), HALF)
    a = z + core * (y - z)
    b = y + core * (z - y)
    piece = core * 16 + a * 4 + b

    def rows(first, count):
        return pl.ds(pl.multiple_of(first * 48, 48), count * 48)

    mine = m_ref.at[:, rows(piece, 1), :]
    first = remote(mine, mo.at[:, rows(piece, 1), cols], ms.at[0], mr.at[0], (g, 1 - h))
    first.start()
    kcopy = remote(k_ref, ko.at[h], ms.at[1], mr.at[1], (g, 1 - h))
    kcopy.start()

    sends = []
    for t, (src, dst, halo) in enumerate(((x_ref, xo, XH), (e_ref, eo, EH))):
        for p in range(2):
            pair = pl.ds(2 * p, 2)
            sends.append((None, remote(src.at[pair], dst.at[:, halo : halo + BINS, cols], xs.at[t, p, 0], xr.at[t, h, 0], (g, p))))
            sends.append((s < 63, remote(
                src.at[pair, BINS - halo : BINS], dst.at[:, 0:halo, cols], xs.at[t, p, 1], xr.at[t, h, 1], (other(lax.rem(s + 1, 64)), p))))
            sends.append((s > 0, remote(
                src.at[pair, 0:halo], dst.at[:, halo + BINS : 2 * halo + BINS, cols], xs.at[t, p, 2], xr.at[t, h, 2], (other(lax.rem(s + 63, 64)), p))))
    for cond, copy in sends:
        if cond is None:
            copy.start()
        else:
            pl.when(cond)(copy.start)
    local = pltpu.make_async_copy(m_ref, mo.at[:, :, cols], ls.at[0])
    local.start()
    klocal = pltpu.make_async_copy(k_ref, ko.at[h], ls.at[1])
    klocal.start()

    def spread(step, count, start, peer):
        copies = []
        for k in (1, 3, 2):
            copies.append(remote(
                mo.at[:, rows(start, count), opp], mo.at[:, rows(start, count), opp], ms.at[2 + step * 3 + k - 1], mr.at[2 + step * 3 + k - 1], peer(k)))
        for copy in copies:
            copy.start()
        for copy in copies:
            copy.wait_recv()
        return copies

    remote(mine, mo.at[:, rows(piece, 1), opp], ms.at[0], mr.at[0], (g, 1 - h)).wait_recv()
    step1 = spread(0, 1, piece, lambda k: (line(core, low, a, lax.rem(b + k, 4)), h))
    step2 = spread(1, 4, core * 16 + a * 4, lambda k: (line(core, low, lax.rem(a + k, 4), b), h))
    last = remote(mo.at[:, rows(core * 16, 16), opp], mo.at[:, rows(core * 16, 16), opp], ms.at[8], mr.at[8], (s + 1 - 2 * core, h))
    last.start()
    last.wait_recv()

    for t, (src, dst, halo) in enumerate(((x_ref, xo, XH), (e_ref, eo, EH))):
        for c in range(2):
            half = pl.ds(c * HALF, HALF)
            remote(src.at[0:2], dst.at[:, halo : halo + BINS, half], xs.at[t, 0, 0], xr.at[t, c, 0], (g, 0)).wait_recv()
            pl.when(g > 0)(remote(src.at[0:2, 0:halo], dst.at[:, 0:halo, half], xs.at[t, 0, 1], xr.at[t, c, 1], (g, 0)).wait_recv)
            pl.when(g < 63)(remote(src.at[0:2, 0:halo], dst.at[:, 0:halo, half], xs.at[t, 0, 2], xr.at[t, c, 2], (g, 0)).wait_recv)
    kcopy.wait_recv()
    local.wait()
    klocal.wait()
    for cond, copy in sends:
        if cond is None:
            copy.wait_send()
        else:
            pl.when(cond)(copy.wait_send)
    for copy in [first, kcopy, last, *step1, *step2]:
        copy.wait_send()


def gather(x, e, m, k):
    D = pltpu.SemaphoreType.DMA
    return pl.pallas_call(
        in_kernel,
        out_shape=(
            jax.ShapeDtypeStruct((2, BINS + 2 * XH, FULL), bf16),
            jax.ShapeDtypeStruct((2, BINS + 2 * EH, FULL), bf16),
            jax.ShapeDtypeStruct((3, FULL, FULL), bf16),
            jax.ShapeDtypeStruct((2, 9, HALF), f32),
        ),
        in_specs=[ANY] * 4,
        out_specs=(ANY,) * 4,
        scratch_shapes=[D((2, 2, 3)), D((2, 2, 3)), D((9,)), D((9,)), D((2,))],
        compiler_params=pltpu.CompilerParams(has_side_effects=True),
    )(x, e, m, k)


def out_kernel(x_ref, e_ref, g_ref, xo, eo, mg, own, got, part, t1, u1, mid, t2, u2, end, v3, fin, swap, rs, rr, ss, sr, ls):
    s, h, low, z, y, core = place()
    g = other(s)
    a = z + core * (y - z)
    b = y + core * (z - y)
    mate = (s + 1 - 2 * core, h)

    first, loads = [], []
    for p in range(2):
        theirs = pl.ds(pl.multiple_of(p * HALF + (1 - core) * 384, 128), 384)
        ours = pl.ds(pl.multiple_of(p * HALF + core * 384, 128), 384)
        first.append(remote(g_ref.at[:, :, theirs], got.at[pl.ds(3 * p, 3)], ss.at[p], sr.at[p], mate))
        loads.append(pltpu.make_async_copy(g_ref.at[:, :, ours], own.at[pl.ds(3 * p, 3)], ls.at[p]))
    for copy in first + loads:
        copy.start()
    results = []
    for t, (src, dst) in enumerate(((x_ref, xo), (e_ref, eo))):
        for c in range(2):
            results.append(remote(src.at[:, :, pl.ds(c * HALF, HALF)], dst.at[pl.ds(2 * h, 2)], rs.at[t, c], rr.at[t, h], (g, c)))
    for copy in results:
        copy.start()
    for copy in first:
        copy.wait_recv()
    for copy in loads:
        copy.wait()

    def rowblock(r):
        return pl.ds(pl.multiple_of(r * 48, 48), 48)

    for n in range(6):
        @pl.loop(0, 32)
        def _(r):
            zz, yy = lax.rem(r // 4, 4), lax.rem(r, 4)
            total = own[n, rowblock(r), :].astype(f32) + got[n, rowblock(r), :].astype(f32)
            part[n, r // 16, zz + core * (yy - zz), yy + core * (zz - yy)] = total.astype(bf16)

    def relay(view, here, peer, t, u, base, loop):
        at = [lax.rem(here + k, 4) for k in range(4)]
        copies = [
            remote(view(0, 3, at[2]), t.at[0], ss.at[base], sr.at[base], peer(at[1])),
            remote(view(3, 3, at[2]), t.at[1], ss.at[base + 1], sr.at[base + 1], peer(at[3])),
        ]
        for copy in copies:
            copy.start()
        more = []
        for side, k in ((0, 1), (1, 3)):
            copies[side].wait_recv()
            loop(lambda i, j: add(view(3 * side, 3, at[k]), t.at[side], i, j), 3)
            more.append(remote(view(0, 6, at[k]), u.at[side], ss.at[base + 2 + side], sr.at[base + 2 + side], peer(at[k])))
            more[-1].start()
        for copy in more:
            copy.wait_recv()
        return copies + more

    def add(dst, src, i, j):
        dst[i, j] = (dst[i, j].astype(f32) + src[i, j].astype(f32)).astype(bf16)

    def loop1(fn, n):
        for i in range(n):
            @pl.loop(0, 8)
            def _(j):
                fn((i, j // 4, lax.rem(j, 4)), None)

    def add1(dst, src, i, j):
        dst[i] = (dst[i].astype(f32) + src[i].astype(f32)).astype(bf16)

    add = add1
    sent = relay(lambda lo, n, d: part.at[pl.ds(lo, n), :, :, d], b, lambda d: (line(core, low, a, d), h), t1, u1, 2, loop1)

    for n in range(6):
        @pl.loop(0, 8)
        def _(j):
            i, q = j // 4, lax.rem(j, 4)
            total = part[n, i, q, b].astype(f32) + u1[0, n, i, q].astype(f32) + u1[1, n, i, q].astype(f32)
            mid[n, i, q] = total.astype(bf16)

    def loop2(fn, n):
        for i in range(n):
            for j in range(2):
                fn((i, j), None)

    sent += relay(lambda lo, n, d: mid.at[pl.ds(lo, n), :, d], a, lambda d: (line(core, low, d, b), h), t2, u2, 6, loop2)
    for n in range(6):
        for i in range(2):
            total = mid[n, i, a].astype(f32) + u2[0, n, i].astype(f32) + u2[1, n, i].astype(f32)
            end[n, i] = total.astype(bf16)

    here = 2 * h + low
    direct = []
    for k in (1, 3, 2):
        d = lax.rem(here + k, 4)
        dh, dl = d // 2, lax.rem(d, 2)
        direct.append(remote(end.at[pl.ds(3 * dh, 3), dl], v3.at[k - 1], ss.at[10 + k - 1], sr.at[10 + k - 1], (dl * 32 + z * 8 + y * 2 + core, dh)))
    for copy in direct:
        copy.start()
    for copy in direct:
        copy.wait_recv()
    for n in range(3):
        fin[n] = end[3 * h + n, low].astype(f32) + v3[0, n].astype(f32) + v3[1, n].astype(f32) + v3[2, n].astype(f32)
    keep = pl.ds(pl.multiple_of(core * 24, 8), 24)
    give = pl.ds(pl.multiple_of((1 - core) * 24, 8), 24)
    final = remote(fin.at[:, give], swap, ss.at[13], sr.at[13], mate)
    final.start()
    mg[:, :, pl.ds(pl.multiple_of(core * 384, 128), 384)] = fin[:, keep, :]
    final.wait_recv()
    mg[:, :, pl.ds(pl.multiple_of((1 - core) * 384, 128), 384)] = swap[...]

    for t, (src, dst) in enumerate(((x_ref, xo), (e_ref, eo))):
        for c in range(2):
            remote(src.at[:, :, 0:HALF], dst.at[pl.ds(2 * c, 2)], rs.at[t, 0], rr.at[t, c], (g, 0)).wait_recv()
    for copy in results + first + sent + direct + [final]:
        copy.wait_send()


def scatter(x, e, grads):
    D = pltpu.SemaphoreType.DMA
    V = pltpu.VMEM
    return pl.pallas_call(
        out_kernel,
        out_shape=(
            jax.ShapeDtypeStruct((4, BINS, HALF), bf16),
            jax.ShapeDtypeStruct((4, BINS, HALF), bf16),
            jax.ShapeDtypeStruct((3, 24, HALF), f32),
        ),
        in_specs=[ANY] * 3,
        out_specs=(ANY, ANY, pl.BlockSpec(memory_space=pltpu.VMEM)),
        scratch_shapes=[
            V((6, FULL, 384), bf16), V((6, FULL, 384), bf16), V((6, 2, 4, 4, 48, 384), bf16),
            V((2, 3, 2, 4, 48, 384), bf16), V((2, 6, 2, 4, 48, 384), bf16), V((6, 2, 4, 48, 384), bf16),
            V((2, 3, 2, 48, 384), bf16), V((2, 6, 2, 48, 384), bf16), V((6, 2, 48, 384), bf16),
            V((3, 3, 48, 384), bf16), V((3, 48, 384), f32), V((3, 24, 384), f32),
            D((2, 2)), D((2, 2)), D((14,)), D((14,)), D((2,)),
        ],
        compiler_params=pltpu.CompilerParams(has_side_effects=True, vmem_limit_bytes=56 << 20),
    )(x, e, grads)


def gelu_parts(pre):
    half = 0.5 * (1.0 + lax.erf(pre * 0.7071067811865476))
    return pre * half, half + pre * jnp.exp(-0.5 * pre * pre) * 0.3989422804014327


def taps(value, d):
    n = value.shape[1]
    wide = jnp.pad(value.astype(f32), ((0, 0), (d, d), (0, 0)))
    return wide[:, 0:n], wide[:, d : d + n], wide[:, 2 * d : 2 * d + n]


def on_device(inputs, kernels, mixers, cotangent):
    s = lax.axis_index("seq")
    g = other(s)
    xg, eg, mix, kg = gather(inputs, cotangent, mixers, kernels.reshape(9, HALF))
    kernel = jnp.concatenate([kg[0], kg[1]], axis=1).reshape(3, 3, FULL)

    def inside(halo):
        at = g * BINS - halo + jnp.arange(BINS + 2 * halo)
        return ((at >= 0) & (at < 64 * BINS))[None, :, None]

    xin, ein = inside(XH), inside(EH)
    zero = jnp.zeros((), bf16)
    x = jnp.where(xin, xg, zero)
    own = slice(XH, XH + BINS)
    acts, slopes = [], []
    for blk, d in enumerate(dilations):
        lowt, midt, hight = taps(x, d)
        pre = kernel[blk, 0] * lowt + kernel[blk, 1] * midt + kernel[blk, 2] * hight
        act, slope = gelu_parts(pre)
        act = act.astype(bf16)
        acts.append(act[:, own].reshape(-1, FULL))
        slopes.append(slope[:, XH - EH : XH + BINS + EH])
        if blk == 2:
            act, x = act[:, own], x[:, own]
        n = act.shape[1]
        mixed = jnp.dot(act.reshape(-1, FULL), mix[blk], preferred_element_type=f32).reshape(2, n, FULL)
        x = (x.astype(f32) + mixed).astype(bf16)
        if blk < 2:
            x = jnp.where(xin, x, zero)
    out = x
    e = jnp.where(ein, eg, zero)
    grads = [None] * 3
    mine = slice(EH, EH + BINS)
    for blk in (2, 1, 0):
        d = dilations[blk]
        flat = e.reshape(-1, FULL)
        back = jnp.einsum("rj,cj->rc", flat, mix[blk], preferred_element_type=f32).reshape(e.shape)
        slope = jnp.where(ein, (back * slopes[blk]).astype(bf16), zero)
        grads[blk] = (
            jnp.einsum("rc,rj->cj", acts[blk], e[:, mine].reshape(-1, FULL), preferred_element_type=f32) * (1.0 / 256.0)
        ).astype(bf16)
        lowt, midt, hight = taps(slope, d)
        e = (e.astype(f32) + kernel[blk, 0] * hight + kernel[blk, 1] * midt + kernel[blk, 2] * lowt).astype(bf16)
    return scatter(out, e[:, mine], jnp.stack(grads))


def solution(mesh):
    return jax.shard_map(
        on_device,
        mesh=mesh,
        in_specs=(P(None, "seq", "ch"), P(None, None, "ch"), P(None, None, "ch"), P(None, "seq", "ch")),
        out_specs=(P(None, "seq", "ch"), P(None, "seq", "ch"), P(None, "seq", "ch")),
        check_vma=False,
    )
```

time: 784 us -> 391 us (0.50)
  waiting for transfers between devices: 632 us -> 0 us
  Pallas kernels: 0 us -> 313 us
  starting transfers between devices: 35.4 us -> 0 us
  matrix products: 53.6 us -> 37.4 us
  between operations: 14.5 us -> 0.94 us
  other arithmetic: 37.8 us -> 25.2 us
  local copies, waits for them, and re-layouts: 4.24 us -> 14.5 us
    reduce_scatter x4 -> x0, waiting for transfers between devices: 500 us -> none  [the longest x1 287 us: on_device(): lax.psum_scatter(jnp.stack(grad_list), 'seq', scatter_dimension=1, tiled=...]
    pallas_call x0 -> x2, Pallas kernels: none -> 313 us  [the longest x1 228 us: gather(): pl.pallas_call(in_kernel, out_shape=(jax.ShapeDtypeStruct((2, BINS + 2 *...]
    all_gather x3 -> x0, waiting for transfers between devices: 128 us -> none  [mixing(): lax.all_gather(act.reshape(seqs * length, chans), 'ch', axis=1, tiled=True)]
    ppermute x12 -> x0, starting transfers between devices: 35 us -> none  [the longest x6 18.5 us: padded_2(): lax.ppermute(lax.slice_in_dim(block, block.shape[dim] - width, None, axis...]
    dot_general x9, matrix products: 53.6 us -> 37.4 us  [the longest x3 18.4 us: on_device(): jnp.einsum('rj,cj->rc', flat, mix[blk], preferred_element_type=f32)]
    convert_element_type x15 -> x7, other arithmetic: 26.7 us -> 17.2 us  [the longest x3 9.86 us: on_device(): act = act.astype(bf16)]
    unnamed x26 -> x34, local copies, waits for them, and re-layouts: 2.36 us -> 11.1 us
  transfers between devices with their start and end apart: 19 -> 0, of which waited for: 11 -> 0; matrix products, arithmetic and copies ran while one was open for 9% -> 0% of each run, Pallas kernels for 0% -> 0%
where the time goes in v1:
time: 391 us
  Pallas kernels  313 us (80%)
  matrix products  37.4 us (10%)
  other arithmetic  25.2 us (6%)
  local copies, waits for them, and re-layouts  14.5 us (4%)
    pallas_call x1, Pallas kernels, gather(): pl.pallas_call(in_kernel, out_shape=(jax.ShapeDtypeStruct((2, BINS + 2 *...  228 us
    pallas_call x1, Pallas kernels, scatter(): pl.pallas_call(out_kernel, out_shape=(jax.ShapeDtypeStruct((4, BINS, HALF...  84.5 us
    dot_general x3, matrix products, on_device(): jnp.einsum('rj,cj->rc', flat, mix[blk], preferred_element_type=f32)  18.4 us
    unnamed x34, local copies, waits for them, and re-layouts  11.1 us
    dot_general x3, matrix products, on_device(): jnp.dot(act.reshape(-1, FULL), mix[blk], preferred_element_type=f32)  10.3 us
    convert_element_type x3, other arithmetic, on_device(): act = act.astype(bf16)  9.86 us
    dot_general x3, matrix products, on_device(): jnp.einsum('rc,rj->cj', acts[blk], e[:, mine].reshape(-1, FULL), preferre...  8.74 us

profile of v1, /device:TPU:1, one launch (start us, length us, event | category | flops | bytes accessed | tf_op | source)
XLA Modules:
  0.0 390.7 jit_solution(4322168060735874515)
XLA Ops:
  0.6 1.4 reshape.58.k_ref
  2.0 228.1 %shard_map.67 = (bf16[2,320,1536]{2,1,0:T(8,128)(2,1)}, bf16[2,288,1536]{2,1,0:T(8,128)(2,1)}, bf16[3,1536,1536]{2,1,0:T(8,128)(2,1)}, f32[2,9,768]{2,1,0:T(8,128)}) custom-call(bf16[4,256,768]{2,1,0:T(8,128)(2,1)} %x_ref.1, bf16[4,256,768]{2,1,0:T(8,128)(2,1)} %e_ref.1, bf16[3,1536,768]{2,1,0:T(8,128)(2,1)} %m_ref.1, f32[9,768]{1,0:T(8,128)} %reshape.58.k_ref), custom_call_target="tpu_custom_call" | custom-call | tf_op jit(solution)/shard_map/pallas_call | solution.py:116
  231.2 2.0 select_convert_fusion
  233.2 4.9 %multiply_convert_fusion.1 = (bf16[2,320,1536]{2,1,0:T(8,128)(2,1)S(1)}, f32[2,320,1536]{2,1,0:T(8,128)}, f32[2,320,1536]{2,1,0:T(8,128)}) fusion(f32[1536]{0:T(1024)S(1)} %get-tuple-element.17, f32[2,320,1536]{2,1,0:T(8,128)S(1)} %select_convert_fusion, f32[1536]{0:T(1024)S(1)} %get-tuple-element.18, f32[1536]{0:T(1024)S(1)} %get-tuple-element.19), kind=kLoop, calls=%fused_computation.43 | loop fusion | flops 9830400 | bytes 13780992 | tf_op jit(solution)/shard_map/convert_element_type | solution.py:298
  238.1 2.2 copy-done.14
  241.1 3.4 fusion.76
  244.5 4.2 %multiply_convert_fusion = (bf16[2,320,1536]{2,1,0:T(8,128)(2,1)S(1)}, f32[2,320,1536]{2,1,0:T(8,128)}, f32[2,320,1536]{2,1,0:T(8,128)}) fusion(f32[1536]{0:T(1024)S(1)} %get-tuple-element.14, f32[2,320,1536]{2,1,0:T(8,128)S(1)} %fusion.76, f32[1536]{0:T(1024)S(1)} %get-tuple-element.15, f32[1536]{0:T(1024)S(1)} %get-tuple-element.16), kind=kLoop, calls=%fused_computation.39 | loop fusion | flops 9830400 | bytes 13780992 | tf_op jit(solution)/shard_map/convert_element_type | solution.py:298
  248.7 3.3 fusion.113
  252.0 1.6 add_multiply_fusion
  254.3 1.2 copy-done
  256.6 3.7 fusion.70.x_ref
  260.3 7.8 %fusion.97 = f32[2,288,1536]{2,1,0:T(8,128)S(1)} fusion(f32[2,320,1536]{2,1,0:T(8,128)} %copy-done.1, f32[2,320,1536]{2,1,0:T(8,128)} %copy-done, bf16[3,1536,1536]{2,1,0:T(8,128)(2,1)} %get-tuple-element.9, pred[288]{0:T(512)(128)(4,1)S(1)} %fusion.110, bf16[2,288,1536]{2,1,0:T(8,128)(2,1)S(1)} %copy-done.2), kind=kOutput, calls=%fused_computation.94 | convolution fusion | flops 2726756352 | bytes 17105920 | tf_op jit(solution)/shard_map/rj,cj->rc/dot_general | solution.py:315
  268.1 1.8 fusion.32
  270.2 5.4 %fusion.91 = f32[2,288,1536]{2,1,0:T(8,128)S(1)} fusion(f32[2,320,1536]{2,1,0:T(8,128)S(1)} %copy-done.6, f32[2,320,1536]{2,1,0:T(8,128)S(1)} %copy-done.5, bf16[2,288,1536]{2,1,0:T(8,128)(2,1)S(1)} %fusion.32, bf16[3,1536,1536]{2,1,0:T(8,128)(2,1)} %get-tuple-element.9, pred[288]{0:T(512)(128)(4,1)S(1)} %fusion.110), kind=kOutput, calls=%fused_computation.92 | convolution fusion | flops 2725871616 | bytes 17105184 | tf_op jit(solution)/shard_map/rj,cj->rc/dot_general | solution.py:315
  275.6 1.1 add_convert_fusion.2
  277.7 5.2 %fusion.85 = f32[2,288,1536]{2,1,0:T(8,128)S(1)} fusion(f32[2,320,1536]{2,1,0:T(8,128)S(1)} %copy-done.4, f32[2,320,1536]{2,1,0:T(8,128)S(1)} %copy-done.3, bf16[2,288,1536]{2,1,0:T(8,128)(2,1)S(1)} %add_convert_fusion.2, bf16[3,1536,1536]{2,1,0:T(8,128)(2,1)} %get-tuple-element.9, pred[288]{0:T(512)(128)(4,1)S(1)} %fusion.110), kind=kOutput, calls=%fused_computation.90 | convolution fusion | flops 2725871616 | bytes 17105184 | tf_op jit(solution)/shard_map/rj,cj->rc/dot_general | solution.py:315
  283.9 2.5 fusion.66.e_ref
  286.5 2.9 fusion.5
  289.5 2.9 fusion.4
  292.4 2.9 fusion.3
  295.3 6.2 %pad_maximum_fusion.g_ref = bf16[3,1536,1536]{2,1,0:T(8,128)(2,1)} fusion(bf16[1,1536,1536]{2,1,0:T(8,128)(2,1)S(1)} %fusion.5, bf16[1,1536,1536]{2,1,0:T(8,128)(2,1)S(1)} %fusion.4, bf16[1,1536,1536]{2,1,0:T(8,128)(2,1)S(1)} %fusion.3), kind=kLoop, calls=%fused_computation | loop fusion | flops 14155776 | bytes 28311552 | tf_op jit(solution)/shard_map/stack | solution.py:322
  301.5 84.5 %shard_map.68 = (bf16[4,256,768]{2,1,0:T(8,128)(2,1)}, bf16[4,256,768]{2,1,0:T(8,128)(2,1)}, f32[3,24,768]{2,1,0:T(8,128)}) custom-call(bf16[2,256,1536]{2,1,0:T(8,128)(2,1)} %fusion.70.x_ref, bf16[2,256,1536]{2,1,0:T(8,128)(2,1)} %fusion.66.e_ref, bf16[3,1536,1536]{2,1,0:T(8,128)(2,1)} %pad_maximum_fusion.g_ref), custom_call_target="tpu_custom_call" | custom-call | tf_op jit(solution)/shard_map/pallas_call | solution.py:248
  386.1 2.8 copy.20
  388.9 1.1 copy.21
  (40 shorter events, 6.8 us)
Async XLA Ops:
  231.2 9.1 %copy-start.14 = (bf16[3,1536,1536]{2,1,0:T(8,128)(2,1)S(1)}, bf16[3,1536,1536]{2,1,0:T(8,128)(2,1)}, u32[]{:S(2)}) copy-start(bf16[3,1536,1536]{2,1,0:T(8,128)(2,1)} %get-tuple-element.9) | copy-start | bytes 42467332
  233.2 7.9 %copy-start.9 = (bf16[2,320,1536]{2,1,0:T(8,128)(2,1)S(1)}, bf16[2,320,1536]{2,1,0:T(8,128)(2,1)}, u32[]{:S(2)}) copy-start(bf16[2,320,1536]{2,1,0:T(8,128)(2,1)} %get-tuple-element.7) | copy-start | bytes 5898244
  238.1 6.3 %copy-start.7 = (bf16[2,320,1536]{2,1,0:T(8,128)(2,1)}, bf16[2,320,1536]{2,1,0:T(8,128)(2,1)S(1)}, u32[]{:S(2)}) copy-start(bf16[2,320,1536]{2,1,0:T(8,128)(2,1)S(1)} %get-tuple-element.25) | copy-start | bytes 5898244
  248.7 3.3 copy-start.10
  253.6 2.0 copy-start
  253.6 3.0 copy-start.1
  256.6 3.7 copy-start.2
  260.3 9.6 %copy-start.6 = (f32[2,320,1536]{2,1,0:T(8,128)S(1)}, f32[2,320,1536]{2,1,0:T(8,128)}, u32[]{:S(2)}) copy-start(f32[2,320,1536]{2,1,0:T(8,128)} %get-tuple-element.24) | copy-start | bytes 11796484
  268.1 2.1 copy-start.5
  270.2 6.5 %copy-start.4 = (f32[2,320,1536]{2,1,0:T(8,128)S(1)}, f32[2,320,1536]{2,1,0:T(8,128)}, u32[]{:S(2)}) copy-start(f32[2,320,1536]{2,1,0:T(8,128)} %get-tuple-element.27) | copy-start | bytes 11796484
  275.6 2.1 copy-start.3
  286.5 2.9 copy-start.11
  289.4 2.9 copy-start.8
  386.0 2.8 copy-start.12
  386.1 3.9 %copy-start.13 = (f32[3,24,768]{2,1,0:T(8,128)S(1)}, f32[3,24,768]{2,1,0:T(8,128)}, u32[]{:S(2)}) copy-start(f32[3,24,768]{2,1,0:T(8,128)} %get-tuple-element.39) | copy-start | bytes 663556

commit v2 on v1

--- a/solution.py
+++ b/solution.py
@@ -38,7 +38,7 @@
     )
 
 
-def in_kernel(x_ref, e_ref, m_ref, k_ref, xo, eo, mo, ko, xs, xr, ms, mr, ls):
+def in_kernel(x_ref, e_ref, m_ref, k_ref, xo, eo, mo, ko, buf, xs, xr, ms, mr, ls):
     s, h, low, z, y, core = place()
     g = other(s)
     cols = pl.ds(pl.multiple_of(h * HALF, HALF), HALF)
@@ -70,10 +70,14 @@
             copy.start()
         else:
             pl.when(cond)(copy.start)
-    local = pltpu.make_async_copy(m_ref, mo.at[:, :, cols], ls.at[0])
-    local.start()
+    load = pltpu.make_async_copy(m_ref, buf, ls.at[0])
+    load.start()
     klocal = pltpu.make_async_copy(k_ref, ko.at[h], ls.at[1])
     klocal.start()
+
+    load.wait()
+    local = pltpu.make_async_copy(buf, mo.at[:, :, cols], ls.at[0])
+    local.start()
 
     def spread(step, count, start, peer):
         copies = []
@@ -123,7 +127,7 @@
         ),
         in_specs=[ANY] * 4,
         out_specs=(ANY,) * 4,
-        scratch_shapes=[D((2, 2, 3)), D((2, 2, 3)), D((9,)), D((9,)), D((2,))],
+        scratch_shapes=[pltpu.VMEM((3, FULL, HALF), bf16), D((2, 2, 3)), D((2, 2, 3)), D((9,)), D((9,)), D((2,))],
         compiler_params=pltpu.CompilerParams(has_side_effects=True),
     )(x, e, m, k)
 

time: 391 us -> 222 us (0.57)
  Pallas kernels: 313 us -> 143 us
    pallas_call x1, Pallas kernels: 228 us -> 62.9 us  [gather(): pl.pallas_call(in_kernel, out_shape=(jax.ShapeDtypeStruct((2, BINS + 2 *...]
    pallas_call x1, Pallas kernels: 84.5 us -> 80.4 us  [scatter(): pl.pallas_call(out_kernel, out_shape=(jax.ShapeDtypeStruct((4, BINS, HALF...]
where the time goes in v2:
time: 222 us; the launch traced here: 221 us
  Pallas kernels  143 us (64%)
  matrix products  37.4 us (17%)
  other arithmetic  25.2 us (11%)
  local copies, waits for them, and re-layouts  14.5 us (7%)
    pallas_call x1, Pallas kernels, scatter(): pl.pallas_call(out_kernel, out_shape=(jax.ShapeDtypeStruct((4, BINS, HALF...  80.4 us
    pallas_call x1, Pallas kernels, gather(): pl.pallas_call(in_kernel, out_shape=(jax.ShapeDtypeStruct((2, BINS + 2 *...  62.9 us
    dot_general x3, matrix products, on_device(): jnp.einsum('rj,cj->rc', flat, mix[blk], preferred_element_type=f32)  18.4 us
    unnamed x34, local copies, waits for them, and re-layouts  11.1 us
    dot_general x3, matrix products, on_device(): jnp.dot(act.reshape(-1, FULL), mix[blk], preferred_element_type=f32)  10.3 us
    convert_element_type x3, other arithmetic, on_device(): act = act.astype(bf16)  9.86 us
    dot_general x3, matrix products, on_device(): jnp.einsum('rc,rj->cj', acts[blk], e[:, mine].reshape(-1, FULL), preferre...  8.74 us
    another operation x1, other arithmetic, on_device(): return scatter(out, e[:, mine], jnp.stack(grads))  6.2 us

profile of v2, /device:TPU:1, one launch (start us, length us, event | category | flops | bytes accessed | tf_op | source)
XLA Modules:
  0.0 221.5 jit_solution(14383342397572620378)
XLA Ops:
  0.6 1.4 reshape.58.k_ref
  2.0 62.9 %shard_map.67 = (bf16[2,320,1536]{2,1,0:T(8,128)(2,1)}, bf16[2,288,1536]{2,1,0:T(8,128)(2,1)}, bf16[3,1536,1536]{2,1,0:T(8,128)(2,1)}, f32[2,9,768]{2,1,0:T(8,128)}) custom-call(bf16[4,256,768]{2,1,0:T(8,128)(2,1)} %x_ref.1, bf16[4,256,768]{2,1,0:T(8,128)(2,1)} %e_ref.1, bf16[3,1536,768]{2,1,0:T(8,128)(2,1)} %m_ref.1, f32[9,768]{1,0:T(8,128)} %reshape.58.k_ref), custom_call_target="tpu_custom_call" | custom-call | tf_op jit(solution)/shard_map/pallas_call | solution.py:120
  66.1 2.0 select_convert_fusion
  68.1 4.9 %multiply_convert_fusion.1 = (bf16[2,320,1536]{2,1,0:T(8,128)(2,1)S(1)}, f32[2,320,1536]{2,1,0:T(8,128)}, f32[2,320,1536]{2,1,0:T(8,128)}) fusion(f32[1536]{0:T(1024)S(1)} %get-tuple-element.17, f32[2,320,1536]{2,1,0:T(8,128)S(1)} %select_convert_fusion, f32[1536]{0:T(1024)S(1)} %get-tuple-element.18, f32[1536]{0:T(1024)S(1)} %get-tuple-element.19), kind=kLoop, calls=%fused_computation.43 | loop fusion | flops 9830400 | bytes 13780992 | tf_op jit(solution)/shard_map/convert_element_type | solution.py:302
  73.0 2.2 copy-done.14
  76.0 3.4 %fusion.76 = f32[2,320,1536]{2,1,0:T(8,128)S(1)} fusion(bf16[2,320,1536]{2,1,0:T(8,128)(2,1)S(1)} %get-tuple-element.25, bf16[3,1536,1536]{2,1,0:T(8,128)(2,1)S(1)} %copy-done.14, pred[320]{0:T(512)(128)(4,1)S(1)} %fusion.109, bf16[2,320,1536]{2,1,0:T(8,128)(2,1)S(1)} %copy-done.9), kind=kOutput, calls=%fused_computation.87 | convolution fusion | flops 3025797120 | bytes 12583424 | tf_op jit(solution)/shard_map/dot_general | solution.py:308
  79.3 4.2 %multiply_convert_fusion = (bf16[2,320,1536]{2,1,0:T(8,128)(2,1)S(1)}, f32[2,320,1536]{2,1,0:T(8,128)}, f32[2,320,1536]{2,1,0:T(8,128)}) fusion(f32[1536]{0:T(1024)S(1)} %get-tuple-element.14, f32[2,320,1536]{2,1,0:T(8,128)S(1)} %fusion.76, f32[1536]{0:T(1024)S(1)} %get-tuple-element.15, f32[1536]{0:T(1024)S(1)} %get-tuple-element.16), kind=kLoop, calls=%fused_computation.39 | loop fusion | flops 9830400 | bytes 13780992 | tf_op jit(solution)/shard_map/convert_element_type | solution.py:302
  83.5 3.3 %fusion.113 = (f32[2,320,1536]{2,1,0:T(8,128)S(1)}, bf16[2,320,1536]{2,1,0:T(8,128)(2,1)S(1)}) fusion(f32[2,320,1536]{2,1,0:T(8,128)S(1)} %fusion.76, bf16[2,320,1536]{2,1,0:T(8,128)(2,1)S(1)} %get-tuple-element.22, bf16[3,1536,1536]{2,1,0:T(8,128)(2,1)S(1)} %copy-done.14, pred[320]{0:T(512)(128)(4,1)S(1)} %fusion.109), kind=kOutput, calls=%fused_computation.122 | convolution fusion | flops 3023831040 | bytes 16515584 | tf_op jit(solution)/shard_map/dot_general | solution.py:308
  86.8 1.6 add_multiply_fusion
  89.2 1.2 copy-done
  91.5 3.7 %fusion.70.x_ref = bf16[2,256,1536]{2,1,0:T(8,128)(2,1)} fusion(bf16[2,256,1536]{2,1,0:T(8,128)(2,1)S(1)} %fusion.69, bf16[3,1536,1536]{2,1,0:T(8,128)(2,1)S(1)} %copy-done.14, bf16[2,320,1536]{2,1,0:T(8,128)(2,1)S(1)} %get-tuple-element.33), kind=kOutput, calls=%fused_computation.85 | convolution fusion | flops 2418278400 | bytes 9437184 | tf_op jit(solution)/shard_map/dot_general | solution.py:308
  95.2 7.8 %fusion.97 = f32[2,288,1536]{2,1,0:T(8,128)S(1)} fusion(f32[2,320,1536]{2,1,0:T(8,128)} %copy-done.1, f32[2,320,1536]{2,1,0:T(8,128)} %copy-done, bf16[3,1536,1536]{2,1,0:T(8,128)(2,1)} %get-tuple-element.9, pred[288]{0:T(512)(128)(4,1)S(1)} %fusion.110, bf16[2,288,1536]{2,1,0:T(8,128)(2,1)S(1)} %copy-done.2), kind=kOutput, calls=%fused_computation.94 | convolution fusion | flops 2726756352 | bytes 17105920 | tf_op jit(solution)/shard_map/rj,cj->rc/dot_general | solution.py:319
  103.0 1.8 fusion.32
  105.1 5.4 %fusion.91 = f32[2,288,1536]{2,1,0:T(8,128)S(1)} fusion(f32[2,320,1536]{2,1,0:T(8,128)S(1)} %copy-done.6, f32[2,320,1536]{2,1,0:T(8,128)S(1)} %copy-done.5, bf16[2,288,1536]{2,1,0:T(8,128)(2,1)S(1)} %fusion.32, bf16[3,1536,1536]{2,1,0:T(8,128)(2,1)} %get-tuple-element.9, pred[288]{0:T(512)(128)(4,1)S(1)} %fusion.110), kind=kOutput, calls=%fused_computation.92 | convolution fusion | flops 2725871616 | bytes 17105184 | tf_op jit(solution)/shard_map/rj,cj->rc/dot_general | solution.py:319
  110.5 1.1 add_convert_fusion.2
  112.6 5.2 %fusion.85 = f32[2,288,1536]{2,1,0:T(8,128)S(1)} fusion(f32[2,320,1536]{2,1,0:T(8,128)S(1)} %copy-done.4, f32[2,320,1536]{2,1,0:T(8,128)S(1)} %copy-done.3, bf16[2,288,1536]{2,1,0:T(8,128)(2,1)S(1)} %add_convert_fusion.2, bf16[3,1536,1536]{2,1,0:T(8,128)(2,1)} %get-tuple-element.9, pred[288]{0:T(512)(128)(4,1)S(1)} %fusion.110), kind=kOutput, calls=%fused_computation.90 | convolution fusion | flops 2725871616 | bytes 17105184 | tf_op jit(solution)/shard_map/rj,cj->rc/dot_general | solution.py:319
  118.7 2.5 %fusion.66.e_ref = bf16[2,256,1536]{2,1,0:T(8,128)(2,1)} fusion(f32[2,288,1536]{2,1,0:T(8,128)S(1)} %get-tuple-element.29, f32[2,288,1536]{2,1,0:T(8,128)S(1)} %fusion.85, f32[2,288,1536]{2,1,0:T(8,128)S(1)} %get-tuple-element.28, f32[1536]{0:T(1024)S(1)} %get-tuple-element.17, f32[1536]{0:T(1024)S(1)} %get-tuple-element.18, f32[1536]{0:T(1024)S(1)} %get-tuple-element.19, ...), kind=kLoop, calls=%fused_computation.78 | loop fusion | flops 6291456 | bytes 12601344 | tf_op jit(solution)/shard_map/convert_element_type | solution.py:325
  121.4 2.9 %fusion.5 = bf16[1,1536,1536]{2,1,0:T(8,128)(2,1)S(1)} fusion(bf16[2,256,1536]{2,1,0:T(8,128)(2,1)S(1)} %fusion.69, bf16[2,288,1536]{2,1,0:T(8,128)(2,1)S(1)} %broadcast_select_fusion), kind=kOutput, calls=%fused_computation.9 | convolution fusion | flops 2420637696 | bytes 7864320 | tf_op jit(solution)/shard_map/rc,rj->cj/dot_general | solution.py:322
  124.3 2.9 %fusion.4 = bf16[1,1536,1536]{2,1,0:T(8,128)(2,1)S(1)} fusion(bf16[2,288,1536]{2,1,0:T(8,128)(2,1)S(1)} %fusion.32, bf16[2,320,1536]{2,1,0:T(8,128)(2,1)S(1)} %copy-done.11), kind=kOutput, calls=%fused_computation.8 | convolution fusion | flops 2420637696 | bytes 7864320 | tf_op jit(solution)/shard_map/rc,rj->cj/dot_general | solution.py:322
  127.3 2.9 %fusion.3 = bf16[1,1536,1536]{2,1,0:T(8,128)(2,1)S(1)} fusion(bf16[2,320,1536]{2,1,0:T(8,128)(2,1)S(1)} %copy-done.8, bf16[2,288,1536]{2,1,0:T(8,128)(2,1)S(1)} %add_convert_fusion.2), kind=kOutput, calls=%fused_computation.7 | convolution fusion | flops 2420637696 | bytes 7864320 | tf_op jit(solution)/shard_map/rc,rj->cj/dot_general | solution.py:322
  130.2 6.2 %pad_maximum_fusion.g_ref = bf16[3,1536,1536]{2,1,0:T(8,128)(2,1)} fusion(bf16[1,1536,1536]{2,1,0:T(8,128)(2,1)S(1)} %fusion.5, bf16[1,1536,1536]{2,1,0:T(8,128)(2,1)S(1)} %fusion.4, bf16[1,1536,1536]{2,1,0:T(8,128)(2,1)S(1)} %fusion.3), kind=kLoop, calls=%fused_computation | loop fusion | flops 14155776 | bytes 28311552 | tf_op jit(solution)/shard_map/stack | solution.py:326
  136.4 80.4 %shard_map.68 = (bf16[4,256,768]{2,1,0:T(8,128)(2,1)}, bf16[4,256,768]{2,1,0:T(8,128)(2,1)}, f32[3,24,768]{2,1,0:T(8,128)}) custom-call(bf16[2,256,1536]{2,1,0:T(8,128)(2,1)} %fusion.70.x_ref, bf16[2,256,1536]{2,1,0:T(8,128)(2,1)} %fusion.66.e_ref, bf16[3,1536,1536]{2,1,0:T(8,128)(2,1)} %pad_maximum_fusion.g_ref), custom_call_target="tpu_custom_call" | custom-call | tf_op jit(solution)/shard_map/pallas_call | solution.py:252
  216.8 2.8 %copy.20 = bf16[4,256,768]{2,1,0:T(8,128)(2,1)} copy(bf16[4,256,768]{2,1,0:T(8,128)(2,1)} %get-tuple-element.37) | data formatting | bytes 3145728
  219.6 1.1 copy.21
  (40 shorter events, 6.8 us)
Async XLA Ops:
  66.1 9.1 %copy-start.14 = (bf16[3,1536,1536]{2,1,0:T(8,128)(2,1)S(1)}, bf16[3,1536,1536]{2,1,0:T(8,128)(2,1)}, u32[]{:S(2)}) copy-start(bf16[3,1536,1536]{2,1,0:T(8,128)(2,1)} %get-tuple-element.9) | copy-start | bytes 42467332
  68.1 7.9 %copy-start.9 = (bf16[2,320,1536]{2,1,0:T(8,128)(2,1)S(1)}, bf16[2,320,1536]{2,1,0:T(8,128)(2,1)}, u32[]{:S(2)}) copy-start(bf16[2,320,1536]{2,1,0:T(8,128)(2,1)} %get-tuple-element.7) | copy-start | bytes 5898244
  73.0 6.3 %copy-start.7 = (bf16[2,320,1536]{2,1,0:T(8,128)(2,1)}, bf16[2,320,1536]{2,1,0:T(8,128)(2,1)S(1)}, u32[]{:S(2)}) copy-start(bf16[2,320,1536]{2,1,0:T(8,128)(2,1)S(1)} %get-tuple-element.25) | copy-start | bytes 5898244
  83.5 3.3 %copy-start.10 = (bf16[2,320,1536]{2,1,0:T(8,128)(2,1)}, bf16[2,320,1536]{2,1,0:T(8,128)(2,1)S(1)}, u32[]{:S(2)}) copy-start(bf16[2,320,1536]{2,1,0:T(8,128)(2,1)S(1)} %get-tuple-element.22) | copy-start | bytes 5898244
  88.4 2.0 copy-start
  88.4 3.0 %copy-start.1 = (f32[2,320,1536]{2,1,0:T(8,128)}, f32[2,320,1536]{2,1,0:T(8,128)S(1)}, u32[]{:S(2)}) copy-start(f32[2,320,1536]{2,1,0:T(8,128)S(1)} %get-tuple-element.21) | copy-start | bytes 11796484
  91.5 3.7 %copy-start.2 = (bf16[2,288,1536]{2,1,0:T(8,128)(2,1)S(1)}, bf16[2,288,1536]{2,1,0:T(8,128)(2,1)}, u32[]{:S(2)}) copy-start(bf16[2,288,1536]{2,1,0:T(8,128)(2,1)} %get-tuple-element.10) | copy-start | bytes 5308420
  95.2 9.6 %copy-start.6 = (f32[2,320,1536]{2,1,0:T(8,128)S(1)}, f32[2,320,1536]{2,1,0:T(8,128)}, u32[]{:S(2)}) copy-start(f32[2,320,1536]{2,1,0:T(8,128)} %get-tuple-element.24) | copy-start | bytes 11796484
  103.0 2.1 copy-start.5
  105.1 6.5 %copy-start.4 = (f32[2,320,1536]{2,1,0:T(8,128)S(1)}, f32[2,320,1536]{2,1,0:T(8,128)}, u32[]{:S(2)}) copy-start(f32[2,320,1536]{2,1,0:T(8,128)} %get-tuple-element.27) | copy-start | bytes 11796484
  110.5 2.1 copy-start.3
  121.4 2.9 %copy-start.11 = (bf16[2,320,1536]{2,1,0:T(8,128)(2,1)S(1)}, bf16[2,320,1536]{2,1,0:T(8,128)(2,1)}, u32[]{:S(2)}) copy-start(bf16[2,320,1536]{2,1,0:T(8,128)(2,1)} %copy-done.10) | copy-start | bytes 5898244
  124.3 2.9 %copy-start.8 = (bf16[2,320,1536]{2,1,0:T(8,128)(2,1)S(1)}, bf16[2,320,1536]{2,1,0:T(8,128)(2,1)}, u32[]{:S(2)}) copy-start(bf16[2,320,1536]{2,1,0:T(8,128)(2,1)} %copy-done.7) | copy-start | bytes 5898244
  216.8 2.8 %copy-start.12 = (bf16[4,256,768]{2,1,0:T(8,128)(2,1)S(1)}, bf16[4,256,768]{2,1,0:T(8,128)(2,1)}, u32[]{:S(2)}) copy-start(bf16[4,256,768]{2,1,0:T(8,128)(2,1)} %get-tuple-element.38) | copy-start | bytes 4718596
  216.8 3.9 %copy-start.13 = (f32[3,24,768]{2,1,0:T(8,128)S(1)}, f32[3,24,768]{2,1,0:T(8,128)}, u32[]{:S(2)}) copy-start(f32[3,24,768]{2,1,0:T(8,128)} %get-tuple-element.39) | copy-start | bytes 663556

commit v3 on v0

v3 whole, which is shorter than its diff:
```python
import jax
import jax.numpy as jnp
from jax import lax
from jax.experimental import pallas as pl
from jax.experimental.pallas import tpu as pltpu
from jax.sharding import PartitionSpec as P

dilations = (2, 4, 8)
MESH = pl.DeviceIdType.MESH
ANY = pl.BlockSpec(memory_space=pl.ANY)
bf16, f32 = jnp.bfloat16, jnp.float32
XH, EH = 32, 16
BINS, HALF, FULL = 256, 768, 1536
XN, EN = BINS + 2 * XH, BINS + 2 * EH
ROWS = 48
TILE = 128


def place():
    s = lax.axis_index("seq")
    h = lax.axis_index("ch")
    core = lax.rem(s, 2)
    y = lax.rem(s // 2, 4)
    z = lax.rem(s // 8, 4)
    return s, h, s // 32, z, y, core


def other(s):
    return lax.rem(s + 32, 64)


def line(core, low, a, b):
    z = a + core * (b - a)
    y = b + core * (a - b)
    return low * 32 + z * 8 + y * 2 + core


def remote(src, dst, send, recv, to):
    return pltpu.make_async_remote_copy(
        src_ref=src, dst_ref=dst, send_sem=send, recv_sem=recv, device_id=to, device_id_type=MESH
    )


def lanes(start, size, step=128):
    return pl.ds(pl.multiple_of(start, step), size)


def body(
    x_ref, e_ref, m_ref, k_ref, xo, eo, mg,
    xv, ev, acts, slopes, down, mv, kv, give, got, part, t1, u1, mid, t2, u2, end, v3, fin, swap,
    xs, xr, ms, mr, ks, rs, rr, ss, sr, ls,
):
    s, h, low, z, y, core = place()
    g = other(s)
    a = z + core * (y - z)
    b = y + core * (z - y)
    mate = (s + 1 - 2 * core, h)
    here = 2 * h + low
    piece = core * 16 + a * 4 + b
    pending = []

    def start(copy, cond=None):
        pending.append((cond, copy))
        if cond is None:
            copy.start()
        else:
            pl.when(cond)(copy.start)
        return copy

    along_a = lambda k: (line(core, low, lax.rem(a + k, 4), b), h)
    along_b = lambda k: (line(core, low, a, lax.rem(b + k, 4)), h)

    def along_x(k):
        d = lax.rem(here + k, 4)
        return (lax.rem(d, 2) * 32 + z * 8 + y * 2 + core, d // 2)

    barrier = pltpu.get_barrier_semaphore()
    peers = [(g, 0), (g, 1), (s, 1 - h), mate]
    peers += [(lax.rem(g + d, 64), p) for d in (1, 63) for p in range(2)]
    peers += [line_of(k) for line_of in (along_a, along_b) for k in (1, 2, 3)]
    for peer in peers:
        pl.semaphore_signal(barrier, inc=1, device_id=peer, device_id_type=MESH)
    own_mix = pltpu.make_async_copy(m_ref, mv.at[:, h], ls.at[0])
    own_mix.start()
    pl.semaphore_wait(barrier, len(peers))

    def rows(first, count):
        return pl.ds(pl.multiple_of(first * ROWS, ROWS), count * ROWS)

    def hop(blk):
        return remote(m_ref.at[blk, rows(piece, 1), :], mv.at[blk, h, rows(piece, 1)], ms.at[blk, 0], mr.at[blk, 0], (g, 1 - h))

    sides = ((x_ref, xv, XH), (e_ref, ev, EH))

    def send_in(t, q):
        src, dst, halo = sides[t]
        cols = lanes(h * HALF, HALF)
        for p in range(2):
            at = (t, q, p)
            start(remote(src.at[2 * p + q], dst.at[q, halo : halo + BINS, cols], xs.at[*at, 0], xr.at[t, q, h, 0], (g, p)))
        for p in range(2):
            at = (t, q, p)
            start(remote(src.at[2 * p + q, BINS - halo : BINS], dst.at[q, 0:halo, cols], xs.at[*at, 1], xr.at[t, q, h, 1], (other(lax.rem(s + 1, 64)), p)), s < 63)
            start(remote(src.at[2 * p + q, 0:halo], dst.at[q, halo + BINS : BINS + 2 * halo, cols], xs.at[*at, 2], xr.at[t, q, h, 2], (other(lax.rem(s + 63, 64)), p)), s > 0)

    def wait_in(t, q):
        src, dst, halo = sides[t]
        for c in range(2):
            half = pl.ds(c * HALF, HALF)
            remote(src.at[0], dst.at[q, halo : halo + BINS, half], xs.at[t, q, 0, 0], xr.at[t, q, c, 0], (g, 0)).wait_recv()
            pl.when(g > 0)(remote(src.at[0, 0:halo], dst.at[q, 0:halo, half], xs.at[t, q, 0, 1], xr.at[t, q, c, 1], (g, 0)).wait_recv)
            pl.when(g < 63)(remote(src.at[0, 0:halo], dst.at[q, halo + BINS : BINS + 2 * halo, half], xs.at[t, q, 0, 2], xr.at[t, q, c, 2], (g, 0)).wait_recv)

    def spread(blk, step, first, count, peer):
        for k in (1, 3, 2):
            at = (blk, step * 3 + k)
            start(remote(mv.at[blk, 1 - h, rows(first, count)], mv.at[blk, 1 - h, rows(first, count)], ms.at[*at], mr.at[*at], peer(k)))

    def spread_wait(blk, step, count, peer):
        for k in (1, 3, 2):
            at = (blk, step * 3 + k)
            remote(mv.at[blk, 1 - h, 0 : count * ROWS], mv.at[blk, 1 - h, 0 : count * ROWS], ms.at[*at], mr.at[*at], peer(k)).wait_recv()

    def across(blk):
        at = mv.at[blk, 1 - h, rows(core * 16, 16)]
        return remote(at, at, ms.at[blk, 7], mr.at[blk, 7], mate)

    start(hop(0))
    kcopy = start(remote(k_ref, kv.at[h], ks.at[0], ks.at[1], (g, 1 - h)))
    klocal = pltpu.make_async_copy(k_ref, kv.at[h], ls.at[1])
    klocal.start()
    send_in(0, 0)
    start(hop(1))
    start(hop(2))
    send_in(0, 1)
    send_in(1, 0)
    send_in(1, 1)
    for blk in range(3):
        hop(blk).wait_recv()
        spread(blk, 0, piece, 1, along_b)
    for blk in range(3):
        spread_wait(blk, 0, 1, along_b)
        spread(blk, 1, core * 16 + a * 4, 4, along_a)

    def zero_edges(ref, q, halo):
        pl.when(g == 0)(lambda: put_zero(ref, q, 0, halo))
        pl.when(g == 63)(lambda: put_zero(ref, q, BINS + halo, halo))

    def put_zero(ref, q, first, count):
        ref[q, first : first + count, :] = jnp.zeros((count, FULL), bf16)

    for q in range(2):
        zero_edges(xv, q, XH)
        zero_edges(ev, q, EH)

    def weight(blk, tap, part_of, at):
        return kv[part_of, 3 * blk + tap : 3 * blk + tap + 1, lanes(at * TILE, TILE)]

    def column_tiles(fn):
        for part_of in range(2):
            @pl.loop(0, HALF // TILE)
            def _(j):
                fn(part_of, j, lanes(part_of * HALF + j * TILE, TILE))

    def forward(blk, q):
        d = dilations[blk]

        def tile(part_of, j, cols):
            value = xv[q, :, cols].astype(f32)
            pre = (
                weight(blk, 0, part_of, j) * pltpu.roll(value, d, 0)
                + weight(blk, 1, part_of, j) * value
                + weight(blk, 2, part_of, j) * pltpu.roll(value, XN - d, 0)
            )
            half = 0.5 * (1.0 + lax.erf(pre * 0.7071067811865476))
            acts[blk, q, :, cols] = (pre * half).astype(bf16)
            slope = half + pre * jnp.exp(-0.5 * pre * pre) * 0.3989422804014327
            slopes[blk, q, :, cols] = slope[XH - EH : XH + BINS + EH].astype(bf16)

        column_tiles(tile)

    def mix(blk, q):
        span = pl.ds(0, XN) if blk < 2 else pl.ds(XH, BINS)
        for part_of in range(2):
            @pl.loop(0, HALF // 256)
            def _(j):
                cols = lanes(part_of * HALF + j * 256, 256)
                mixed = jnp.dot(acts[blk, q, span, :], mv[blk, part_of, :, lanes(j * 256, 256)], preferred_element_type=f32)
                xv[q, span, cols] = (xv[q, span, cols].astype(f32) + mixed).astype(bf16)
        if blk < 2:
            zero_edges(xv, q, XH)

    def back(blk, q):
        @pl.loop(0, FULL // 256)
        def _(j):
            span = pl.ds(pl.multiple_of(j * 256, 256), 256)
            total = None
            for part_of in range(2):
                term = lax.dot_general(
                    ev[q, :, part_of * HALF : (part_of + 1) * HALF], mv[blk, part_of, span, :],
                    (((1,), (1,)), ((), ())), preferred_element_type=f32)
                total = term if total is None else total + term
            cols = lanes(j * 256, 256)
            down[q, :, cols] = (total * slopes[blk, q, :, cols].astype(f32)).astype(bf16)
        zero_edges(down, q, EH)

    def lower(blk, q):
        d = dilations[blk]

        def tile(part_of, j, cols):
            value = down[q, :, cols].astype(f32)
            total = (
                ev[q, :, cols].astype(f32)
                + weight(blk, 0, part_of, j) * pltpu.roll(value, EN - d, 0)
                + weight(blk, 1, part_of, j) * value
                + weight(blk, 2, part_of, j) * pltpu.roll(value, d, 0)
            )
            ev[q, :, cols] = total.astype(bf16)

        column_tiles(tile)

    def grads(blk):
        scale = 1.0 / 256.0
        for keep in (0, 1):
            theirs = core if keep else 1 - core
            for p in range(2):
                cols = lanes(p * HALF + theirs * 384, 384)

                @pl.loop(0, 4)
                def _(c):
                    total = None
                    for q in range(2):
                        term = lax.dot_general(
                            acts[blk, q, XH : XH + BINS, lanes(c * 384, 384)], ev[q, EH : EH + BINS, cols],
                            (((0,), (0,)), ((), ())), preferred_element_type=f32)
                        total = term if total is None else total + term
                    total = (total * scale).astype(bf16)
                    for r in range(8):
                        zz, yy = lax.rem(2 * c + r // 4, 4), r % 4
                        block = total[r * ROWS : (r + 1) * ROWS]
                        if keep:
                            part[blk, p, c // 2, zz + core * (yy - zz), yy + core * (zz - yy)] = block
                        else:
                            give[p, c // 2, zz + (1 - core) * (yy - zz), yy + (1 - core) * (zz - yy)] = block

    def add(dst, src):
        dst[...] = (dst[...].astype(f32) + src[...].astype(f32)).astype(bf16)

    def send(blk, n, src, dst, to):
        return start(remote(src, dst, ss.at[blk, n], sr.at[blk, n], to))

    def recv(blk, n, dst):
        remote(dst, dst, ss.at[blk, n], sr.at[blk, n], mate).wait_recv()

    pos = lambda here_, k: lax.rem(here_ + k, 4)

    def step0(blk):
        remote(give, got.at[blk], ss.at[blk, 0], sr.at[blk, 0], mate).start()

    def step1(blk):
        recv(blk, 0, got.at[blk])
        for p in range(2):
            @pl.loop(0, 32)
            def _(r):
                add(part.at[blk, p, r // 16, lax.rem(r // 4, 4), lax.rem(r, 4)], got.at[blk, p, r // 16, lax.rem(r // 4, 4), lax.rem(r, 4)])
        send(blk, 1, part.at[blk, 0, :, :, pos(b, 2)], t1.at[blk, 0], along_b(1))
        send(blk, 2, part.at[blk, 1, :, :, pos(b, 2)], t1.at[blk, 1], along_b(3))

    def step2(blk):
        for side, k in ((0, 1), (1, 3)):
            recv(blk, 1 + side, t1.at[blk, side])
            @pl.loop(0, 8)
            def _(r):
                add(part.at[blk, side, r // 4, lax.rem(r, 4), pos(b, k)], t1.at[blk, side, r // 4, lax.rem(r, 4)])
            send(blk, 3 + side, part.at[blk, :, :, :, pos(b, k)], u1.at[blk, side], along_b(k))

    def step3(blk):
        recv(blk, 3, u1.at[blk, 0])
        recv(blk, 4, u1.at[blk, 1])
        for p in range(2):
            @pl.loop(0, 8)
            def _(r):
                i, j = r // 4, lax.rem(r, 4)
                total = part[blk, p, i, j, b].astype(f32) + u1[blk, 0, p, i, j].astype(f32) + u1[blk, 1, p, i, j].astype(f32)
                mid[blk, p, i, j] = total.astype(bf16)
        send(blk, 5, mid.at[blk, 0, :, pos(a, 2)], t2.at[blk, 0], along_a(1))
        send(blk, 6, mid.at[blk, 1, :, pos(a, 2)], t2.at[blk, 1], along_a(3))

    def step4(blk):
        for side, k in ((0, 1), (1, 3)):
            recv(blk, 5 + side, t2.at[blk, side])
            for i in range(2):
                add(mid.at[blk, side, i, pos(a, k)], t2.at[blk, side, i])
            send(blk, 7 + side, mid.at[blk, :, :, pos(a, k)], u2.at[blk, side], along_a(k))

    def step5(blk):
        recv(blk, 7, u2.at[blk, 0])
        recv(blk, 8, u2.at[blk, 1])
        for p in range(2):
            for i in range(2):
                total = mid[blk, p, i, a].astype(f32) + u2[blk, 0, p, i].astype(f32) + u2[blk, 1, p, i].astype(f32)
                end[blk, p, i] = total.astype(bf16)
        for k in (1, 3, 2):
            d = pos(here, k)
            send(blk, 8 + k, end.at[blk, d // 2, lax.rem(d, 2)], v3.at[blk, k - 1], along_x(k))

    def step6(blk):
        for k in (1, 3, 2):
            recv(blk, 8 + k, v3.at[blk, k - 1])
        fin[blk] = end[blk, h, low].astype(f32) + v3[blk, 0].astype(f32) + v3[blk, 1].astype(f32) + v3[blk, 2].astype(f32)
        send(blk, 12, fin.at[blk, pl.ds(pl.multiple_of((1 - core) * 24, 8), 24)], swap.at[blk], mate)

    def step7(blk):
        mg[blk, :, lanes(core * 384, 384)] = fin[blk, pl.ds(pl.multiple_of(core * 24, 8), 24), :]
        recv(blk, 12, swap.at[blk])
        mg[blk, :, lanes((1 - core) * 384, 384)] = swap[blk]

    def give_sent(blk):
        remote(give, got.at[blk], ss.at[blk, 0], sr.at[blk, 0], mate).wait_send()

    def send_out(t, q):
        src, halo, dst = ((xv, XH, xo), (ev, EH, eo))[t]
        for c in range(2):
            start(remote(src.at[q, halo : halo + BINS, c * HALF : (c + 1) * HALF], dst.at[2 * h + q], rs.at[t, q, c], rr.at[t, q, h], (g, c)))

    for q in range(2):
        wait_in(0, q)
        if q == 0:
            klocal.wait()
            remote(k_ref, kv.at[1 - h], ks.at[0], ks.at[1], (g, 1 - h)).wait_recv()
        for blk in range(3):
            forward(blk, q)
            if q == 0:
                if blk == 0:
                    own_mix.wait()
                    for each in range(3):
                        spread_wait(each, 1, 4, along_a)
                        start(across(each))
                remote(mv.at[blk, 1 - h, 0 : 16 * ROWS], mv.at[blk, 1 - h, 0 : 16 * ROWS], ms.at[blk, 7], mr.at[blk, 7], mate).wait_recv()
            mix(blk, q)
        send_out(0, q)

    wait_in(1, 0)
    wait_in(1, 1)
    for blk in (2, 1, 0):
        if blk < 2:
            give_sent(blk + 1)
        grads(blk)
        step0(blk)
        if blk < 2:
            step3(blk + 1)
        if blk < 1:
            step6(blk + 2)
        for q in range(2):
            back(blk, q)
            lower(blk, q)
            if blk == 0:
                send_out(1, q)
            if q == 0:
                step1(blk)
                if blk < 2:
                    step4(blk + 1)
                if blk < 1:
                    step7(blk + 2)
        step2(blk)
        if blk < 2:
            step5(blk + 1)
    step3(0)
    step6(1)
    step4(0)
    step7(1)
    step5(0)
    step6(0)
    step7(0)

    for t, dst in enumerate((xo, eo)):
        for q in range(2):
            for c in range(2):
                remote(xv.at[q, 0:BINS, 0:HALF], dst.at[2 * c + q], rs.at[t, q, 0], rr.at[t, q, c], (g, 0)).wait_recv()
    give_sent(0)
    for cond, copy in pending:
        if cond is None:
            copy.wait_send()
        else:
            pl.when(cond)(copy.wait_send)


def on_device(inputs, kernels, mixers, cotangent):
    D = pltpu.SemaphoreType.DMA
    V = pltpu.VMEM
    return pl.pallas_call(
        body,
        out_shape=(
            jax.ShapeDtypeStruct((4, BINS, HALF), bf16),
            jax.ShapeDtypeStruct((4, BINS, HALF), bf16),
            jax.ShapeDtypeStruct((3, 24, HALF), f32),
        ),
        in_specs=[ANY] * 4,
        out_specs=(ANY, ANY, pl.BlockSpec(memory_space=pltpu.VMEM)),
        scratch_shapes=[
            V((2, XN, FULL), bf16), V((2, EN, FULL), bf16), V((3, 2, XN, FULL), bf16), V((3, 2, EN, FULL), bf16), V((2, EN, FULL), bf16),
            V((3, 2, FULL, HALF), bf16), V((2, 9, HALF), f32),
            V((2, 2, 4, 4, ROWS, 384), bf16), V((3, 2, 2, 4, 4, ROWS, 384), bf16), V((3, 2, 2, 4, 4, ROWS, 384), bf16),
            V((3, 2, 2, 4, ROWS, 384), bf16), V((3, 2, 2, 2, 4, ROWS, 384), bf16), V((3, 2, 2, 4, ROWS, 384), bf16),
            V((3, 2, 2, ROWS, 384), bf16), V((3, 2, 2, 2, ROWS, 384), bf16), V((3, 2, 2, ROWS, 384), bf16),
            V((3, 3, ROWS, 384), bf16), V((3, ROWS, 384), f32), V((3, 24, 384), f32),
            D((2, 2, 2, 3)), D((2, 2, 2, 3)), D((3, 8)), D((3, 8)), D((2,)), D((2, 2, 2)), D((2, 2, 2)), D((3, 13)), D((3, 13)), D((2,)),
        ],
        compiler_params=pltpu.CompilerParams(collective_id=0, has_side_effects=True, vmem_limit_bytes=60 << 20),
    )(inputs, cotangent, mixers, kernels.reshape(9, HALF))


def solution(mesh):
    return jax.shard_map(
        on_device,
        mesh=mesh,
        in_specs=(P(None, "seq", "ch"), P(None, None, "ch"), P(None, None, "ch"), P(None, "seq", "ch")),
        out_specs=(P(None, "seq", "ch"), P(None, "seq", "ch"), P(None, "seq", "ch")),
        check_vma=False,
    )
```

time: 784 us -> 167 us (0.21)
  waiting for transfers between devices: 632 us -> 0 us
  Pallas kernels: 0 us -> 160 us
  matrix products: 53.6 us -> 0 us
  other arithmetic: 37.8 us -> 0 us
  starting transfers between devices: 35.4 us -> 0 us
  between operations: 14.5 us -> 0.65 us
    reduce_scatter x4 -> x0, waiting for transfers between devices: 500 us -> none  [the longest x1 287 us: on_device(): lax.psum_scatter(jnp.stack(grad_list), 'seq', scatter_dimension=1, tiled=...]
    pallas_call x0 -> x1, Pallas kernels: none -> 160 us  [on_device(): pl.pallas_call(body, out_shape=(jax.ShapeDtypeStruct((4, BINS, HALF), bf1...]
    all_gather x3 -> x0, waiting for transfers between devices: 128 us -> none  [mixing(): lax.all_gather(act.reshape(seqs * length, chans), 'ch', axis=1, tiled=True)]
    dot_general x9 -> x0, matrix products: 53.6 us -> none  [the longest x3 19.5 us: on_device(): jnp.einsum('rj,cj->rc', flat, mixers[block], preferred_element_type=jnp.f...]
    ppermute x12 -> x0, starting transfers between devices: 35 us -> none  [the longest x6 18.5 us: padded_2(): lax.ppermute(lax.slice_in_dim(block, block.shape[dim] - width, None, axis...]
    convert_element_type x15 -> x0, other arithmetic: 26.7 us -> none  [the longest x3 10.1 us: on_device(): (back.reshape(seqs, bins, chans) * gelu_slope(pre)).astype(jnp.bfloat16)]
    another operation x1 -> x0, other arithmetic: 11.1 us -> none  [on_device(): jnp.stack(grad_list)]
  transfers between devices with their start and end apart: 19 -> 0, of which waited for: 11 -> 0; matrix products, arithmetic and copies ran while one was open for 9% -> 0% of each run, Pallas kernels for 0% -> 0%
where the time goes in v3:
time: 167 us
  Pallas kernels  160 us (96%)
  local copies, waits for them, and re-layouts  6.01 us (4%)
    pallas_call x1, Pallas kernels, on_device(): pl.pallas_call(body, out_shape=(jax.ShapeDtypeStruct((4, BINS, HALF), bf1...  160 us
    unnamed x7, local copies, waits for them, and re-layouts  4.61 us

profile of v3, /device:TPU:1, one launch (start us, length us, event | category | flops | bytes accessed | tf_op | source)
XLA Modules:
  0.0 167.0 jit_solution(7298185100409566757)
XLA Ops:
  0.6 1.4 reshape.9.k_ref
  2.0 160.3 %shard_map.67 = (bf16[4,256,768]{2,1,0:T(8,128)(2,1)}, bf16[4,256,768]{2,1,0:T(8,128)(2,1)}, f32[3,24,768]{2,1,0:T(8,128)}) custom-call(bf16[4,256,768]{2,1,0:T(8,128)(2,1)} %x_ref.1, bf16[4,256,768]{2,1,0:T(8,128)(2,1)} %e_ref.1, bf16[3,1536,768]{2,1,0:T(8,128)(2,1)} %m_ref.1, f32[9,768]{1,0:T(8,128)} %reshape.9.k_ref), custom_call_target="tpu_custom_call" | custom-call | tf_op jit(solution)/shard_map/pallas_call | solution.py:391
  162.3 0.0 copy-start
  162.3 2.8 %copy.10 = bf16[4,256,768]{2,1,0:T(8,128)(2,1)} copy(bf16[4,256,768]{2,1,0:T(8,128)(2,1)} %get-tuple-element.6) | data formatting | bytes 3145728
  165.1 0.0 copy-done
  165.1 0.0 copy-start.1
  165.1 1.1 copy.11
  166.3 0.0 copy-done.1
  166.3 0.7 copy.12
Async XLA Ops:
  162.3 2.8 %copy-start = (bf16[4,256,768]{2,1,0:T(8,128)(2,1)S(1)}, bf16[4,256,768]{2,1,0:T(8,128)(2,1)}, u32[]{:S(2)}) copy-start(bf16[4,256,768]{2,1,0:T(8,128)(2,1)} %get-tuple-element.7) | copy-start | bytes 4718596
  165.1 1.1 copy-start.1

commit v4 on v3

v4 whole, which is shorter than its diff:
```python
import jax
import jax.numpy as jnp
from jax import lax
from jax.experimental import pallas as pl
from jax.experimental.pallas import tpu as pltpu
from jax.sharding import PartitionSpec as P

dilations = (2, 4, 8)
MESH = pl.DeviceIdType.MESH
ANY = pl.BlockSpec(memory_space=pl.ANY)
bf16, f32 = jnp.bfloat16, jnp.float32
XH, EH = 32, 16
BINS, HALF, FULL = 256, 768, 1536
XN, EN = BINS + 2 * XH, BINS + 2 * EH
ROWS = 48
TILE = 128


def place():
    s = lax.axis_index("seq")
    h = lax.axis_index("ch")
    core = lax.rem(s, 2)
    y = lax.rem(s // 2, 4)
    z = lax.rem(s // 8, 4)
    return s, h, s // 32, z, y, core


def other(s):
    return lax.rem(s + 32, 64)


def line(core, low, a, b):
    z = a + core * (b - a)
    y = b + core * (a - b)
    return low * 32 + z * 8 + y * 2 + core


def remote(src, dst, send, recv, to):
    return pltpu.make_async_remote_copy(
        src_ref=src, dst_ref=dst, send_sem=send, recv_sem=recv, device_id=to, device_id_type=MESH
    )


def lanes(start, size, step=128):
    return pl.ds(pl.multiple_of(start, step), size)


def body(
    x_ref, e_ref, m_ref, k_ref, xo, eo, mg,
    xv, ev, acts, slopes, down, mv, kv, give, got, part, t1, u1, mid, u2, end, v3, fin, swap,
    xs, xr, es, er, ms, mr, ks, rs, rr, ss, sr, ls,
):
    s, h, low, z, y, core = place()
    g = other(s)
    a = z + core * (y - z)
    b = y + core * (z - y)
    mate = (s + 1 - 2 * core, h)
    here = 2 * h + low
    piece = core * 16 + a * 4 + b
    pending = []

    def start(copy, cond=None):
        pending.append((cond, copy))
        if cond is None:
            copy.start()
        else:
            pl.when(cond)(copy.start)
        return copy

    along_a = lambda k: (line(core, low, lax.rem(a + k, 4), b), h)
    along_b = lambda k: (line(core, low, a, lax.rem(b + k, 4)), h)

    def along_x(k):
        d = lax.rem(here + k, 4)
        return (lax.rem(d, 2) * 32 + z * 8 + y * 2 + core, d // 2)

    barrier = pltpu.get_barrier_semaphore()
    peers = [(g, 0), (g, 1), (s, 1 - h), mate]
    peers += [(other(lax.rem(g + d, 64)), h) for d in (1, 63)]
    peers += [line_of(k) for line_of in (along_a, along_b) for k in (1, 2, 3)]
    for peer in peers:
        pl.semaphore_signal(barrier, inc=1, device_id=peer, device_id_type=MESH)
    pl.semaphore_wait(barrier, len(peers))

    def rows(first, count):
        return pl.ds(pl.multiple_of(first * ROWS, ROWS), count * ROWS)

    def hop(blk):
        return remote(m_ref.at[blk, rows(piece, 1), :], mv.at[blk, h, rows(piece, 1)], ms.at[blk, 0], mr.at[blk, 0], (g, 1 - h))

    sides = ((x_ref, xv, XH), (e_ref, ev, EH))

    def send_in(t, q):
        src, dst, halo = sides[t]
        for p in range(2):
            start(remote(src.at[2 * p + q], dst.at[q, halo : halo + BINS, lanes(h * HALF, HALF)], xs.at[t, q, p], xr.at[t, q, h], (g, p)))

    def wait_in(t, q):
        src, dst, halo = sides[t]
        for c in range(2):
            remote(src.at[0], dst.at[q, halo : halo + BINS, c * HALF : (c + 1) * HALF], xs.at[t, q, 0], xr.at[t, q, c], (g, 0)).wait_recv()
        for cond, copy in edges(t, q):
            pl.when(cond)(copy.start)

    def edges(t, q):
        src, dst, halo = sides[t]
        up, down_to = (other(lax.rem(g + 1, 64)), h), (other(lax.rem(g + 63, 64)), h)
        return (
            (g < 63, remote(dst.at[q, BINS : BINS + halo], dst.at[q, 0:halo], es.at[t, q, 0], er.at[t, q, 0], up)),
            (g > 0, remote(dst.at[q, halo : 2 * halo], dst.at[q, halo + BINS : 2 * halo + BINS], es.at[t, q, 1], er.at[t, q, 1], down_to)),
        )

    def edges_sent(t, q):
        for cond, copy in edges(t, q):
            pl.when(cond)(copy.wait_send)

    def wait_edges(t, q):
        src, dst, halo = sides[t]
        pl.when(g > 0)(remote(dst.at[q, 0:halo], dst.at[q, 0:halo], es.at[t, q, 0], er.at[t, q, 0], mate).wait_recv)
        pl.when(g < 63)(remote(dst.at[q, 0:halo], dst.at[q, halo + BINS : 2 * halo + BINS], es.at[t, q, 1], er.at[t, q, 1], mate).wait_recv)

    def spread(blk, step, first, count, peer):
        for k in (1, 3, 2):
            at = (blk, step * 3 + k)
            start(remote(mv.at[blk, 1 - h, rows(first, count)], mv.at[blk, 1 - h, rows(first, count)], ms.at[*at], mr.at[*at], peer(k)))

    def spread_wait(blk, step, count, peer):
        for k in (1, 3, 2):
            at = (blk, step * 3 + k)
            remote(mv.at[blk, 1 - h, 0 : count * ROWS], mv.at[blk, 1 - h, 0 : count * ROWS], ms.at[*at], mr.at[*at], peer(k)).wait_recv()

    def across(blk):
        at = mv.at[blk, 1 - h, rows(core * 16, 16)]
        return remote(at, at, ms.at[blk, 7], mr.at[blk, 7], mate)

    for blk in range(3):
        start(hop(blk))
    send_in(0, 0)
    kcopy = start(remote(k_ref, kv.at[h], ks.at[0], ks.at[1], (g, 1 - h)))
    klocal = pltpu.make_async_copy(k_ref, kv.at[h], ls.at[1])
    klocal.start()
    own_mix = pltpu.make_async_copy(m_ref, mv.at[:, h], ls.at[0])
    own_mix.start()

    def zero_edges(ref, q, halo):
        pl.when(g == 0)(lambda: put_zero(ref, q, 0, halo))
        pl.when(g == 63)(lambda: put_zero(ref, q, BINS + halo, halo))

    def put_zero(ref, q, first, count):
        ref[q, first : first + count, :] = jnp.zeros((count, FULL), bf16)

    for q in range(2):
        zero_edges(xv, q, XH)
        zero_edges(ev, q, EH)

    def weight(blk, tap, part_of, at):
        return kv[part_of, blk, tap : tap + 1, lanes(at * TILE, TILE)]

    def column_tiles(fn):
        for part_of in range(2):
            @pl.loop(0, HALF // TILE)
            def _(j):
                fn(part_of, j, lanes(part_of * HALF + j * TILE, TILE))

    def forward(blk, q):
        d = dilations[blk]

        def tile(part_of, j, cols):
            value = xv[q, :, cols].astype(f32)
            pre = (
                weight(blk, 0, part_of, j) * pltpu.roll(value, d, 0)
                + weight(blk, 1, part_of, j) * value
                + weight(blk, 2, part_of, j) * pltpu.roll(value, XN - d, 0)
            )
            half = 0.5 * (1.0 + lax.erf(pre * 0.7071067811865476))
            acts[blk, q, :, cols] = (pre * half).astype(bf16)
            slope = half + pre * jnp.exp(-0.5 * pre * pre) * 0.3989422804014327
            slopes[blk, q, :, cols] = slope[XH - EH : XH + BINS + EH].astype(bf16)

        column_tiles(tile)

    def mix(blk, q):
        span = pl.ds(0, XN) if blk < 2 else pl.ds(XH, BINS)
        @pl.loop(0, 2)
        def _(part_of):
            cols = lanes(part_of * HALF, HALF)
            mixed = jnp.dot(acts[blk, q, span, :], mv[blk, part_of], preferred_element_type=f32)
            xv[q, span, cols] = (xv[q, span, cols].astype(f32) + mixed).astype(bf16)

        if blk < 2:
            zero_edges(xv, q, XH)

    def back(blk, q):
        total = None
        for part_of in range(2):
            term = lax.dot_general(
                ev[q, :, part_of * HALF : (part_of + 1) * HALF], mv[blk, part_of],
                (((1,), (1,)), ((), ())), preferred_element_type=f32)
            total = term if total is None else total + term
        down[q] = (total * slopes[blk, q].astype(f32)).astype(bf16)
        zero_edges(down, q, EH)

    def lower(blk, q):
        d = dilations[blk]

        def tile(part_of, j, cols):
            value = down[q, :, cols].astype(f32)
            total = (
                ev[q, :, cols].astype(f32)
                + weight(blk, 0, part_of, j) * pltpu.roll(value, EN - d, 0)
                + weight(blk, 1, part_of, j) * value
                + weight(blk, 2, part_of, j) * pltpu.roll(value, d, 0)
            )
            ev[q, :, cols] = total.astype(bf16)

        column_tiles(tile)

    def product(blk, of, c):
        total = None
        for q in range(2):
            right = jnp.concatenate([ev[q, EH : EH + BINS, lanes(p * HALF + of * 384, 384)] for p in range(2)], axis=1)
            term = lax.dot_general(
                acts[blk, q, XH : XH + BINS, lanes(c * HALF, HALF)], right,
                (((0,), (0,)), ((), ())), preferred_element_type=f32)
            total = term if total is None else total + term
        return total * (1.0 / 256.0)

    def spot(of, r):
        zz, yy = r // 4, r % 4
        return zz + of * (yy - zz), yy + of * (zz - yy)

    def grads_give(blk):
        @pl.loop(0, 2)
        def _(c):
            total = product(blk, 1 - core, c).astype(bf16)
            for p in range(2):
                for r in range(16):
                    give[(p, c, *spot(1 - core, r))] = total[r * ROWS : (r + 1) * ROWS, p * 384 : (p + 1) * 384]

        remote(give, got.at[blk], ss.at[blk, 11], sr.at[blk, 11], mate).start()

    def grads_own(blk):
        recv(blk, 11, got.at[blk])

        @pl.loop(0, 2)
        def _(c):
            total = product(blk, core, c)
            for p in range(2):
                for r in range(16):
                    at = (blk, p, c, *spot(core, r))
                    part[at] = (total[r * ROWS : (r + 1) * ROWS, p * 384 : (p + 1) * 384] + got[at].astype(f32)).astype(bf16)

        for p in range(2):
            send(blk, p, part.at[blk, p, :, :, pos(b, 2)], t1.at[blk, p], along_b(1 + 2 * p))

    def add(dst, src):
        dst[...] = (dst[...].astype(f32) + src[...].astype(f32)).astype(bf16)

    def send(blk, n, src, dst, to):
        return start(remote(src, dst, ss.at[blk, n], sr.at[blk, n], to))

    def recv(blk, n, dst):
        remote(dst, dst, ss.at[blk, n], sr.at[blk, n], mate).wait_recv()

    pos = lambda here_, k: lax.rem(here_ + k, 4)

    def step2(blk):
        for side, k in ((0, 1), (1, 3)):
            recv(blk, side, t1.at[blk, side])

            @pl.loop(0, 8)
            def _(r):
                add(part.at[blk, side, r // 4, lax.rem(r, 4), pos(b, k)], t1.at[blk, side, r // 4, lax.rem(r, 4)])

            send(blk, 2 + side, part.at[blk, :, :, :, pos(b, k)], u1.at[blk, side], along_b(k))

    def step3(blk):
        recv(blk, 2, u1.at[blk, 0])
        recv(blk, 3, u1.at[blk, 1])
        for p in range(2):
            @pl.loop(0, 8)
            def _(r):
                i, j = r // 4, lax.rem(r, 4)
                total = part[blk, p, i, j, b].astype(f32) + u1[blk, 0, p, i, j].astype(f32) + u1[blk, 1, p, i, j].astype(f32)
                mid[blk, p, i, j] = total.astype(bf16)
        for k in (2, 1, 3):
            send(blk, 3 + k, mid.at[blk, :, :, pos(a, k)], u2.at[blk, k - 1], along_a(k))

    def step4(blk):
        for k in (1, 3, 2):
            recv(blk, 3 + k, u2.at[blk, k - 1])
        for p in range(2):
            for i in range(2):
                total = mid[blk, p, i, a].astype(f32)
                for k in range(3):
                    total = total + u2[blk, k, p, i].astype(f32)
                end[blk, p, i] = total.astype(bf16)
        for k in (2, 1, 3):
            d = pos(here, k)
            send(blk, 6 + k, end.at[blk, d // 2, lax.rem(d, 2)], v3.at[blk, k - 1], along_x(k))

    def step5(blk):
        for k in (1, 3, 2):
            recv(blk, 6 + k, v3.at[blk, k - 1])
        fin[blk] = end[blk, h, low].astype(f32) + v3[blk, 0].astype(f32) + v3[blk, 1].astype(f32) + v3[blk, 2].astype(f32)
        send(blk, 10, fin.at[blk, pl.ds(pl.multiple_of((1 - core) * 24, 8), 24)], swap.at[blk], mate)

    def step6(blk):
        mg[blk, :, lanes(core * 384, 384)] = fin[blk, pl.ds(pl.multiple_of(core * 24, 8), 24), :]
        recv(blk, 10, swap.at[blk])
        mg[blk, :, lanes((1 - core) * 384, 384)] = swap[blk]

    def give_sent(blk):
        remote(give, got.at[blk], ss.at[blk, 11], sr.at[blk, 11], mate).wait_send()

    def send_out(t, q):
        src, halo, dst = ((xv, XH, xo), (ev, EH, eo))[t]
        for c in range(2):
            start(remote(src.at[q, halo : halo + BINS, c * HALF : (c + 1) * HALF], dst.at[2 * h + q], rs.at[t, q, c], rr.at[t, q, h], (g, c)))

    def crossed(blk):
        remote(mv.at[blk, 1 - h, 0 : 16 * ROWS], mv.at[blk, 1 - h, 0 : 16 * ROWS], ms.at[blk, 7], mr.at[blk, 7], mate).wait_recv()

    for blk in range(3):
        hop(blk).wait_recv()
        spread(blk, 0, piece, 1, along_b)
    spread_wait(0, 0, 1, along_b)
    spread(0, 1, core * 16 + a * 4, 4, along_a)
    spread_wait(1, 0, 1, along_b)
    spread_wait(2, 0, 1, along_b)
    wait_in(0, 0)
    send_in(0, 1)
    klocal.wait()
    remote(k_ref, kv.at[1 - h], ks.at[0], ks.at[1], (g, 1 - h)).wait_recv()
    spread_wait(0, 1, 4, along_a)
    start(across(0))
    spread(1, 1, core * 16 + a * 4, 4, along_a)
    wait_edges(0, 0)
    forward(0, 0)
    own_mix.wait()
    crossed(0)
    edges_sent(0, 0)
    mix(0, 0)
    forward(1, 0)
    spread_wait(1, 1, 4, along_a)
    start(across(1))
    spread(2, 1, core * 16 + a * 4, 4, along_a)
    wait_in(0, 1)
    send_in(1, 0)
    crossed(1)
    mix(1, 0)
    forward(2, 0)
    wait_edges(0, 1)
    forward(0, 1)
    edges_sent(0, 1)
    mix(0, 1)
    spread_wait(2, 1, 4, along_a)
    start(across(2))
    forward(1, 1)
    wait_in(1, 0)
    send_in(1, 1)
    mix(1, 1)
    crossed(2)
    mix(2, 0)
    forward(2, 1)
    mix(2, 1)

    wait_edges(1, 0)
    back(2, 0)
    wait_in(1, 1)
    send_out(0, 0)
    send_out(0, 1)
    grads_give(2)
    wait_edges(1, 1)
    back(2, 1)
    grads_own(2)
    edges_sent(1, 0)
    lower(2, 0)
    edges_sent(1, 1)
    lower(2, 1)
    give_sent(2)
    grads_give(1)
    step2(2)
    back(1, 0)
    grads_own(1)
    back(1, 1)
    lower(1, 0)
    lower(1, 1)
    give_sent(1)
    grads_give(0)
    step3(2)
    back(0, 0)
    step2(1)
    grads_own(0)
    lower(0, 0)
    send_out(1, 0)
    back(0, 1)
    lower(0, 1)
    step4(2)
    send_out(1, 1)
    step3(1)
    step2(0)
    step5(2)
    step4(1)
    step6(2)
    step5(1)
    step3(0)
    step6(1)
    step4(0)
    step5(0)
    step6(0)
    give_sent(0)

    for t, dst in enumerate((xo, eo)):
        for q in range(2):
            for c in range(2):
                remote(xv.at[q, 0:BINS, 0:HALF], dst.at[2 * c + q], rs.at[t, q, 0], rr.at[t, q, c], (g, 0)).wait_recv()
    for cond, copy in pending:
        if cond is None:
            copy.wait_send()
        else:
            pl.when(cond)(copy.wait_send)


def on_device(inputs, kernels, mixers, cotangent):
    D = pltpu.SemaphoreType.DMA
    V = pltpu.VMEM
    return pl.pallas_call(
        body,
        out_shape=(
            jax.ShapeDtypeStruct((4, BINS, HALF), bf16),
            jax.ShapeDtypeStruct((4, BINS, HALF), bf16),
            jax.ShapeDtypeStruct((3, 24, HALF), f32),
        ),
        in_specs=[ANY] * 4,
        out_specs=(ANY, ANY, pl.BlockSpec(memory_space=pltpu.VMEM)),
        scratch_shapes=[
            V((2, XN, FULL), bf16), V((2, EN, FULL), bf16), V((3, 2, XN, FULL), bf16), V((3, 2, EN, FULL), bf16), V((2, EN, FULL), bf16),
            V((3, 2, FULL, HALF), bf16), V((2, 3, 3, HALF), f32),
            V((2, 2, 4, 4, ROWS, 384), bf16), V((3, 2, 2, 4, 4, ROWS, 384), bf16), V((3, 2, 2, 4, 4, ROWS, 384), bf16),
            V((3, 2, 2, 4, ROWS, 384), bf16), V((3, 2, 2, 2, 4, ROWS, 384), bf16), V((3, 2, 2, 4, ROWS, 384), bf16),
            V((3, 3, 2, 2, ROWS, 384), bf16), V((3, 2, 2, ROWS, 384), bf16),
            V((3, 3, ROWS, 384), bf16), V((3, ROWS, 384), f32), V((3, 24, 384), f32),
            D((2, 2, 2)), D((2, 2, 2)), D((2, 2, 2)), D((2, 2, 2)), D((3, 8)), D((3, 8)), D((2,)), D((2, 2, 2)), D((2, 2, 2)), D((3, 13)), D((3, 13)), D((2,)),
        ],
        compiler_params=pltpu.CompilerParams(collective_id=0, has_side_effects=True, vmem_limit_bytes=60 << 20),
    )(inputs, cotangent, mixers, kernels)


def solution(mesh):
    return jax.shard_map(
        on_device,
        mesh=mesh,
        in_specs=(P(None, "seq", "ch"), P(None, None, "ch"), P(None, None, "ch"), P(None, "seq", "ch")),
        out_specs=(P(None, "seq", "ch"), P(None, "seq", "ch"), P(None, "seq", "ch")),
        check_vma=False,
    )
```

time: 167 us -> 135 us (0.81)
  the two profiles are of different devices: /device:TPU:1 before, /device:TPU:41 now
where the time goes in v4:
time: 135 us
  Pallas kernels  129 us (96%)
  local copies, waits for them, and re-layouts  4.61 us (3%)
    pallas_call x1, Pallas kernels, on_device(): pl.pallas_call(body, out_shape=(jax.ShapeDtypeStruct((4, BINS, HALF), bf1...  129 us
    unnamed x7, local copies, waits for them, and re-layouts  4.61 us

profile of v4, /device:TPU:41, one launch (start us, length us, event | category | flops | bytes accessed | tf_op | source)
XLA Modules:
  0.0 134.5 jit_solution(6719085419488251448)
XLA Ops:
  0.6 129.3 %shard_map.67 = (bf16[4,256,768]{2,1,0:T(8,128)(2,1)}, bf16[4,256,768]{2,1,0:T(8,128)(2,1)}, f32[3,24,768]{2,1,0:T(8,128)}) custom-call(bf16[4,256,768]{2,1,0:T(8,128)(2,1)} %x_ref.1, bf16[4,256,768]{2,1,0:T(8,128)(2,1)} %e_ref.1, bf16[3,1536,768]{2,1,0:T(8,128)(2,1)} %m_ref.1, f32[3,3,768]{2,1,0:T(4,128)} %k_ref.1), custom_call_target="tpu_custom_call" | custom-call | tf_op jit(solution)/shard_map/pallas_call | solution.py:428
  129.9 0.0 copy-start
  129.9 2.8 %copy.10 = bf16[4,256,768]{2,1,0:T(8,128)(2,1)} copy(bf16[4,256,768]{2,1,0:T(8,128)(2,1)} %get-tuple-element.6) | data formatting | bytes 3145728
  132.7 0.0 copy-done
  132.7 0.0 copy-start.1
  132.7 1.1 copy.11
  133.8 0.0 copy-done.1
  133.8 0.7 copy.12
Async XLA Ops:
  129.9 2.8 %copy-start = (bf16[4,256,768]{2,1,0:T(8,128)(2,1)S(1)}, bf16[4,256,768]{2,1,0:T(8,128)(2,1)}, u32[]{:S(2)}) copy-start(bf16[4,256,768]{2,1,0:T(8,128)(2,1)} %get-tuple-element.7) | copy-start | bytes 4718596
  132.7 1.1 copy-start.1

commit v5 on v4

--- a/solution.py
+++ b/solution.py
@@ -229,29 +229,27 @@
         zz, yy = r // 4, r % 4
         return zz + of * (yy - zz), yy + of * (zz - yy)
 
+    def given(blk, c):
+        return remote(give.at[:, c], got.at[blk, :, c], ss.at[blk, 18 + c], sr.at[blk, 18 + c], mate)
+
     def grads_give(blk):
-        @pl.loop(0, 2)
-        def _(c):
+        for c in range(2):
             total = product(blk, 1 - core, c).astype(bf16)
             for p in range(2):
                 for r in range(16):
                     give[(p, c, *spot(1 - core, r))] = total[r * ROWS : (r + 1) * ROWS, p * 384 : (p + 1) * 384]
-
-        remote(give, got.at[blk], ss.at[blk, 11], sr.at[blk, 11], mate).start()
+            given(blk, c).start()
 
     def grads_own(blk):
-        recv(blk, 11, got.at[blk])
-
-        @pl.loop(0, 2)
-        def _(c):
+        for c in range(2):
+            given(blk, c).wait_recv()
             total = product(blk, core, c)
             for p in range(2):
                 for r in range(16):
                     at = (blk, p, c, *spot(core, r))
                     part[at] = (total[r * ROWS : (r + 1) * ROWS, p * 384 : (p + 1) * 384] + got[at].astype(f32)).astype(bf16)
-
-        for p in range(2):
-            send(blk, p, part.at[blk, p, :, :, pos(b, 2)], t1.at[blk, p], along_b(1 + 2 * p))
+            for p in range(2):
+                send(blk, 2 * p + c, part.at[blk, p, c, :, pos(b, 2)], t1.at[blk, p, c], along_b(1 + 2 * p))
 
     def add(dst, src):
         dst[...] = (dst[...].astype(f32) + src[...].astype(f32)).astype(bf16)
@@ -265,30 +263,32 @@
     pos = lambda here_, k: lax.rem(here_ + k, 4)
 
     def step2(blk):
-        for side, k in ((0, 1), (1, 3)):
-            recv(blk, side, t1.at[blk, side])
-
-            @pl.loop(0, 8)
-            def _(r):
-                add(part.at[blk, side, r // 4, lax.rem(r, 4), pos(b, k)], t1.at[blk, side, r // 4, lax.rem(r, 4)])
-
-            send(blk, 2 + side, part.at[blk, :, :, :, pos(b, k)], u1.at[blk, side], along_b(k))
+        for c in range(2):
+            for side, k in ((0, 1), (1, 3)):
+                recv(blk, 2 * side + c, t1.at[blk, side, c])
+
+                @pl.loop(0, 4)
+                def _(r):
+                    add(part.at[blk, side, c, r, pos(b, k)], t1.at[blk, side, c, r])
+
+                send(blk, 4 + 2 * side + c, part.at[blk, :, c, :, pos(b, k)], u1.at[blk, side, :, c], along_b(k))
 
     def step3(blk):
-        recv(blk, 2, u1.at[blk, 0])
-        recv(blk, 3, u1.at[blk, 1])
-        for p in range(2):
-            @pl.loop(0, 8)
-            def _(r):
-                i, j = r // 4, lax.rem(r, 4)
-                total = part[blk, p, i, j, b].astype(f32) + u1[blk, 0, p, i, j].astype(f32) + u1[blk, 1, p, i, j].astype(f32)
-                mid[blk, p, i, j] = total.astype(bf16)
-        for k in (2, 1, 3):
-            send(blk, 3 + k, mid.at[blk, :, :, pos(a, k)], u2.at[blk, k - 1], along_a(k))
+        for c in range(2):
+            recv(blk, 4 + c, u1.at[blk, 0, :, c])
+            recv(blk, 6 + c, u1.at[blk, 1, :, c])
+            for p in range(2):
+                @pl.loop(0, 4)
+                def _(j):
+                    total = part[blk, p, c, j, b].astype(f32) + u1[blk, 0, p, c, j].astype(f32) + u1[blk, 1, p, c, j].astype(f32)
+                    mid[blk, p, c, j] = total.astype(bf16)
+            for k in (2, 1, 3):
+                send(blk, 6 + 2 * k + c, mid.at[blk, :, c, pos(a, k)], u2.at[blk, k - 1, :, c], along_a(k))
 
     def step4(blk):
         for k in (1, 3, 2):
-            recv(blk, 3 + k, u2.at[blk, k - 1])
+            for c in range(2):
+                recv(blk, 6 + 2 * k + c, u2.at[blk, k - 1, :, c])
         for p in range(2):
             for i in range(2):
                 total = mid[blk, p, i, a].astype(f32)
@@ -297,21 +297,22 @@
                 end[blk, p, i] = total.astype(bf16)
         for k in (2, 1, 3):
             d = pos(here, k)
-            send(blk, 6 + k, end.at[blk, d // 2, lax.rem(d, 2)], v3.at[blk, k - 1], along_x(k))
+            send(blk, 13 + k, end.at[blk, d // 2, lax.rem(d, 2)], v3.at[blk, k - 1], along_x(k))
 
     def step5(blk):
         for k in (1, 3, 2):
-            recv(blk, 6 + k, v3.at[blk, k - 1])
+            recv(blk, 13 + k, v3.at[blk, k - 1])
         fin[blk] = end[blk, h, low].astype(f32) + v3[blk, 0].astype(f32) + v3[blk, 1].astype(f32) + v3[blk, 2].astype(f32)
-        send(blk, 10, fin.at[blk, pl.ds(pl.multiple_of((1 - core) * 24, 8), 24)], swap.at[blk], mate)
+        send(blk, 17, fin.at[blk, pl.ds(pl.multiple_of((1 - core) * 24, 8), 24)], swap.at[blk], mate)
 
     def step6(blk):
         mg[blk, :, lanes(core * 384, 384)] = fin[blk, pl.ds(pl.multiple_of(core * 24, 8), 24), :]
-        recv(blk, 10, swap.at[blk])
+        recv(blk, 17, swap.at[blk])
         mg[blk, :, lanes((1 - core) * 384, 384)] = swap[blk]
 
     def give_sent(blk):
-        remote(give, got.at[blk], ss.at[blk, 11], sr.at[blk, 11], mate).wait_send()
+        for c in range(2):
+            given(blk, c).wait_send()
 
     def send_out(t, q):
         src, halo, dst = ((xv, XH, xo), (ev, EH, eo))[t]
@@ -388,23 +389,23 @@
     lower(1, 1)
     give_sent(1)
     grads_give(0)
+    back(0, 0)
+    grads_own(0)
+    step2(1)
     step3(2)
-    back(0, 0)
-    step2(1)
-    grads_own(0)
     lower(0, 0)
     send_out(1, 0)
     back(0, 1)
     lower(0, 1)
+    send_out(1, 1)
+    step2(0)
     step4(2)
-    send_out(1, 1)
     step3(1)
-    step2(0)
     step5(2)
     step4(1)
     step6(2)
+    step3(0)
     step5(1)
-    step3(0)
     step6(1)
     step4(0)
     step5(0)
@@ -441,7 +442,7 @@
             V((3, 2, 2, 4, ROWS, 384), bf16), V((3, 2, 2, 2, 4, ROWS, 384), bf16), V((3, 2, 2, 4, ROWS, 384), bf16),
             V((3, 3, 2, 2, ROWS, 384), bf16), V((3, 2, 2, ROWS, 384), bf16),
             V((3, 3, ROWS, 384), bf16), V((3, ROWS, 384), f32), V((3, 24, 384), f32),
-            D((2, 2, 2)), D((2, 2, 2)), D((2, 2, 2)), D((2, 2, 2)), D((3, 8)), D((3, 8)), D((2,)), D((2, 2, 2)), D((2, 2, 2)), D((3, 13)), D((3, 13)), D((2,)),
+            D((2, 2, 2)), D((2, 2, 2)), D((2, 2, 2)), D((2, 2, 2)), D((3, 8)), D((3, 8)), D((2,)), D((2, 2, 2)), D((2, 2, 2)), D((3, 20)), D((3, 20)), D((2,)),
         ],
         compiler_params=pltpu.CompilerParams(collective_id=0, has_side_effects=True, vmem_limit_bytes=60 << 20),
     )(inputs, cotangent, mixers, kernels)

time: 135 us -> 128 us (0.948)
  the two profiles are of different devices: /device:TPU:41 before, /device:TPU:1 now
where the time goes in v5:
time: 128 us
  Pallas kernels  123 us (96%)
  local copies, waits for them, and re-layouts  4.61 us (4%)
    pallas_call x1, Pallas kernels, on_device(): pl.pallas_call(body, out_shape=(jax.ShapeDtypeStruct((4, BINS, HALF), bf1...  123 us
    unnamed x7, local copies, waits for them, and re-layouts  4.61 us

profile of v5, /device:TPU:1, one launch (start us, length us, event | category | flops | bytes accessed | tf_op | source)
XLA Modules:
  0.0 128.3 jit_solution(2430786664655582506)
XLA Ops:
  0.6 123.0 %shard_map.67 = (bf16[4,256,768]{2,1,0:T(8,128)(2,1)}, bf16[4,256,768]{2,1,0:T(8,128)(2,1)}, f32[3,24,768]{2,1,0:T(8,128)}) custom-call(bf16[4,256,768]{2,1,0:T(8,128)(2,1)} %x_ref.1, bf16[4,256,768]{2,1,0:T(8,128)(2,1)} %e_ref.1, bf16[3,1536,768]{2,1,0:T(8,128)(2,1)} %m_ref.1, f32[3,3,768]{2,1,0:T(4,128)} %k_ref.1), custom_call_target="tpu_custom_call" | custom-call | tf_op jit(solution)/shard_map/pallas_call | solution.py:429
  123.6 0.0 copy-start
  123.7 2.8 %copy.10 = bf16[4,256,768]{2,1,0:T(8,128)(2,1)} copy(bf16[4,256,768]{2,1,0:T(8,128)(2,1)} %get-tuple-element.6) | data formatting | bytes 3145728
  126.4 0.0 copy-done
  126.4 0.0 copy-start.1
  126.4 1.1 copy.11
  127.6 0.0 copy-done.1
  127.6 0.7 copy.12
Async XLA Ops:
  123.6 2.8 %copy-start = (bf16[4,256,768]{2,1,0:T(8,128)(2,1)S(1)}, bf16[4,256,768]{2,1,0:T(8,128)(2,1)}, u32[]{:S(2)}) copy-start(bf16[4,256,768]{2,1,0:T(8,128)(2,1)} %get-tuple-element.7) | copy-start | bytes 4718596
  126.4 1.1 copy-start.1

commit v6 on v5

--- a/solution.py
+++ b/solution.py
@@ -381,9 +381,9 @@
     lower(2, 1)
     give_sent(2)
     grads_give(1)
-    step2(2)
     back(1, 0)
     grads_own(1)
+    step2(2)
     back(1, 1)
     lower(1, 0)
     lower(1, 1)

time: 128 us -> 128 us (level)
  no operation moved by 1% of the time
where the time goes in v6:
time: 128 us
  Pallas kernels  122 us (95%)
  local copies, waits for them, and re-layouts  4.61 us (4%)
    pallas_call x1, Pallas kernels, on_device(): pl.pallas_call(body, out_shape=(jax.ShapeDtypeStruct((4, BINS, HALF), bf1...  122 us
    unnamed x7, local copies, waits for them, and re-layouts  4.61 us

profile of v6, /device:TPU:1, one launch (start us, length us, event | category | flops | bytes accessed | tf_op | source)
XLA Modules:
  0.0 127.7 jit_solution(15258187308666126259)
XLA Ops:
  0.6 122.5 %shard_map.67 = (bf16[4,256,768]{2,1,0:T(8,128)(2,1)}, bf16[4,256,768]{2,1,0:T(8,128)(2,1)}, f32[3,24,768]{2,1,0:T(8,128)}) custom-call(bf16[4,256,768]{2,1,0:T(8,128)(2,1)} %x_ref.1, bf16[4,256,768]{2,1,0:T(8,128)(2,1)} %e_ref.1, bf16[3,1536,768]{2,1,0:T(8,128)(2,1)} %m_ref.1, f32[3,3,768]{2,1,0:T(4,128)} %k_ref.1), custom_call_target="tpu_custom_call" | custom-call | tf_op jit(solution)/shard_map/pallas_call | solution.py:429
  123.1 0.0 copy-start
  123.1 2.8 %copy.10 = bf16[4,256,768]{2,1,0:T(8,128)(2,1)} copy(bf16[4,256,768]{2,1,0:T(8,128)(2,1)} %get-tuple-element.6) | data formatting | bytes 3145728
  125.9 0.0 copy-done
  125.9 0.0 copy-start.1
  125.9 1.1 copy.11
  127.0 0.0 copy-done.1
  127.0 0.7 copy.12
Async XLA Ops:
  123.1 2.8 %copy-start = (bf16[4,256,768]{2,1,0:T(8,128)(2,1)S(1)}, bf16[4,256,768]{2,1,0:T(8,128)(2,1)}, u32[]{:S(2)}) copy-start(bf16[4,256,768]{2,1,0:T(8,128)(2,1)} %get-tuple-element.7) | copy-start | bytes 4718596
  125.9 1.1 copy-start.1
